TPU v7x, 128 devices: a whole 4x4x4 slice. The times are simulated.
128 devices in a mesh: drift: 8 (over x, core), beam: 16 (over z, y).
Axes of the slice: x: 4, y: 4, z: 4, core: 2. Of those that a mesh axis runs over, the one named last changes fastest.
Arguments:
- features: bfloat16 [64, 32, 256, 128], P('drift', None, 'beam'), may hold values from -6 to 6
- occupied: int32 [8, 32, 16], P('drift', 'beam'), may hold values 0 or 1
- voxel_fragment: int32 [64, 256, 128], P('drift', 'beam'), may hold values from 0 to 4095, as said below
- conv_weight: bfloat16 [32, 864], replicated, may hold values from -0.21875 to 0.21875
- embed_weight: bfloat16 [32, 256], replicated, may hold values from -6 to 6
- message_weight: bfloat16 [256, 256], replicated, may hold values from -0.375 to 0.375
- update_weight: bfloat16 [256, 256], replicated, may hold values from -0.375 to 0.375
- edge_source: int32 [131072], P(('drift', 'beam')), may hold values from 0 to 4095
- edge_target: int32 [131072], P(('drift', 'beam')), may hold values from 0 to 255
- out_cotangent: bfloat16 [32768, 256], P(('drift', 'beam')), may hold values from -6 to 6
Outputs:
- fragment_out: bfloat16 [32768, 256], P(('drift', 'beam'))
- grad_features: float32 [64, 32, 256, 128], P('drift', None, 'beam')
- grad_conv: float32 [32, 864], replicated
Inputs may be any that keep to these rules, and one draw needn't show every extreme that they name: `voxel_fragment`: index among the 4096 fragments of the voxel's drift row.
All inputs are finite; a program needn't handle non-finite values. No bound on the sum of `occupied` on one device may be relied on, other than what follows from the above.
Results may differ from a plain program's by a relative error of at most 0.01.
Values may be sent and summed in bfloat16 or wider, within the bound.
A program may use at most 64 MiB of HBM per device.

v0:
```python
import jax
import jax.numpy as jnp
from jax import lax
from jax.sharding import PartitionSpec as P

BLOCK = 8


def padded_2(cells, sides, width):
    for axis, dim in sides:
        count = lax.axis_size(axis)
        ends = count - 1
        head = lax.slice_in_dim(cells, 0, width, axis=dim)
        tail = lax.slice_in_dim(cells, cells.shape[dim] - width, cells.shape[dim], axis=dim)
        cells = jnp.concatenate(
            [
                lax.ppermute(tail, axis, [(i, (i + 1) % count) for i in range(ends)]),
                cells,
                lax.ppermute(head, axis, [((i + 1) % count, i) for i in range(ends)]),
            ],
            axis=dim,
        )
    return cells


def cut_along(array, dim, size):
    before, after = (array.shape[:dim], array.shape[dim + 1 :])
    return jnp.moveaxis(array.reshape(*before, size, -1, *after), dim, 0)


def sum_at_owner(array, axis, dim):
    tiles = cut_along(array, dim, lax.axis_size(axis))
    arrived = lax.all_to_all(tiles, axis, split_axis=0, concat_axis=0, tiled=True)
    return arrived.sum(axis=0)


def from_everyone(array, axis):
    copies = jnp.broadcast_to(array, (lax.axis_size(axis), *array.shape))
    return lax.all_to_all(copies, axis, split_axis=0, concat_axis=0, tiled=True)


def joined_along(tiles, dim):
    lengths = list(tiles.shape[1:])
    lengths[dim] *= tiles.shape[0]
    return jnp.moveaxis(tiles, 0, dim).reshape(lengths)


def collect(array, axis, dim):
    tiles = from_everyone(array, axis)
    return joined_along(tiles, dim)


def slope(value):
    sig = jax.nn.sigmoid(value)
    return sig * (1.0 + value * (1.0 - sig))


def columns(padded, row):
    channels = padded.shape[1]
    height = padded.shape[2] - 2
    depth = padded.shape[3] - 2
    anchor = jnp.zeros((), jnp.int32)
    pieces = []
    for off_a in range(3):
        for off_b in range(3):
            for off_c in range(3):
                index = (row + off_a, anchor, anchor + off_b, anchor + off_c)
                piece = lax.dynamic_slice(padded, index, (1, channels, height, depth))
                pieces.append(piece.reshape(channels, height * depth))
    return jnp.concatenate(pieces, 0)


def convolve(padded, weight):
    rows = padded.shape[0] - 2
    height = padded.shape[2] - 2
    depth = padded.shape[3] - 2

    def one_row(row):
        return jnp.dot(weight, columns(padded, row), preferred_element_type=jnp.float32)

    result = lax.map(one_row, jnp.arange(rows, dtype=jnp.int32))
    return result.reshape(rows, weight.shape[0], height, depth)


def project_back(embed_full, grad, pre):
    return lax.dot_general(
        embed_full, grad * slope(pre), (((1,), (1,)), ((), ())), precision=lax.Precision.HIGHEST
    )


def embed_rows(pooled, embed_weight):
    return lax.dot_general(
        pooled, embed_weight, (((0,), (0,)), ((), ())), preferred_element_type=jnp.float32
    )


def body(
    features,
    occupied,
    voxel_fragment,
    conv_weight,
    embed_weight,
    message_weight,
    update_weight,
    edge_source,
    edge_target,
    out_cotangent,
):
    f32 = jnp.float32
    rows, channels, height, depth = features.shape
    frag_dev = out_cotangent.shape[0]
    frag_row = frag_dev * lax.axis_size("beam")
    mask = jnp.repeat(jnp.repeat(jnp.repeat(occupied, BLOCK, 0), BLOCK, 1), BLOCK, 2).astype(f32)
    mask_four = mask[:, None]
    active = features * mask_four.astype(jnp.bfloat16)
    rimmed = padded_2(active, (("drift", 0), ("beam", 2)), 1)
    rimmed = jnp.pad(rimmed, ((0, 0), (0, 0), (0, 0), (1, 1)))
    conv_out = convolve(rimmed, conv_weight)
    hidden = mask_four * (active.astype(f32) + jax.nn.silu(conv_out))
    frag_ids = voxel_fragment.reshape(-1)
    by_voxel = hidden.transpose(0, 2, 3, 1).reshape(-1, channels)
    sums = jax.ops.segment_sum(by_voxel, frag_ids, num_segments=frag_row).T
    counts = jax.ops.segment_sum(mask.reshape(-1), frag_ids, num_segments=frag_row)
    sums, counts = (sum_at_owner(sums, "beam", 1), sum_at_owner(counts, "beam", 0))
    divisor = jnp.maximum(counts, 1.0)[None, :]
    pooled = (sums / divisor).astype(jnp.bfloat16)
    pre_own = embed_rows(pooled, embed_weight)
    own = jax.nn.silu(pre_own).astype(jnp.bfloat16)
    pooled_all = collect(pooled, "beam", 1)
    pre_all = embed_rows(pooled_all, embed_weight)
    table = jax.nn.silu(pre_all).astype(jnp.bfloat16)
    sources = jnp.take(table, edge_source, axis=0)
    pre_msg = jnp.dot(sources, message_weight, preferred_element_type=f32)
    messages = jax.nn.silu(pre_msg).astype(jnp.bfloat16)
    gathered = jax.ops.segment_sum(messages.astype(f32), edge_target, num_segments=frag_dev).astype(
        jnp.bfloat16
    )
    fragment_out = (
        own.astype(f32) + jnp.dot(gathered, update_weight, preferred_element_type=f32)
    ).astype(jnp.bfloat16)
    back_agg = jnp.dot(out_cotangent, update_weight.T, preferred_element_type=f32).astype(
        jnp.bfloat16
    )
    back_pre = (jnp.take(back_agg, edge_target, axis=0).astype(f32) * slope(pre_msg)).astype(
        jnp.bfloat16
    )
    back_src = jnp.dot(back_pre, message_weight.T, preferred_element_type=f32)
    back_rows = jax.ops.segment_sum(back_src, edge_source, num_segments=frag_row)
    embed_full = embed_weight.astype(f32)
    remote = sum_at_owner(project_back(embed_full, back_rows, pre_all), "beam", 1)
    back_pooled = remote + project_back(embed_full, out_cotangent.astype(f32), pre_own)
    back_mean = back_pooled / divisor
    mean_all = lax.all_gather(back_mean, "beam", axis=1, tiled=True)
    back_hidden = (
        jnp.take(mean_all, frag_ids, axis=1)
        .reshape(channels, rows, height, depth)
        .transpose(1, 0, 2, 3)
    )
    back_conv = (mask_four * back_hidden * slope(conv_out)).astype(jnp.bfloat16)
    rim_grad = padded_2(back_conv, (("drift", 0), ("beam", 2)), 1)
    rim_grad = jnp.pad(rim_grad, ((0, 0), (0, 0), (0, 0), (1, 1)))
    flipped = (
        conv_weight.reshape(channels, 27, channels)[:, ::-1, :]
        .transpose(2, 1, 0)
        .reshape(channels, 27 * channels)
    )
    back_active = mask_four * back_hidden + convolve(rim_grad, flipped)
    grad_features = mask_four * back_active

    def accumulate(total, row):
        cols = columns(rimmed, row)
        slab = lax.dynamic_index_in_dim(back_conv, row, 0, keepdims=False).reshape(channels, -1)
        term = lax.dot_general(slab, cols, (((1,), (1,)), ((), ())), preferred_element_type=f32)
        return (total + term, None)

    local_grad, _ = lax.scan(
        accumulate, jnp.zeros((channels, 27 * channels), f32), jnp.arange(rows, dtype=jnp.int32)
    )
    grad_conv = lax.psum(local_grad, ("drift", "beam"))
    return (fragment_out, grad_features, grad_conv)


def solution(mesh):
    return jax.shard_map(
        body,
        mesh=mesh,
        in_specs=(
            P("drift", None, "beam", None),
            P("drift", "beam", None),
            P("drift", "beam", None),
            P(),
            P(),
            P(),
            P(),
            P(("drift", "beam")),
            P(("drift", "beam")),
            P(("drift", "beam"), None),
        ),
        out_specs=(P(("drift", "beam"), None), P("drift", None, "beam", None), P()),
        check_vma=False,
    )
```

profile of v0, /device:TPU:1, one launch (start us, length us, event | category | flops | bytes accessed | tf_op | source)
XLA Modules:
  0.0 786.1 jit_solution(11984716983973108843)
XLA Ops:
  8.6 86.8 %scatter_custom_fusion.1 = f32[4096]{0:T(1024)} fusion(s32[16384]{0:T(1024)} %bitcast.886, f32[16384]{0:T(1024)S(1)} %reshape.650, f32[]{:T(128)} %constant.165.clone.1), kind=kCustom, calls=%fused_computation.265 | custom fusion | flops 16384 | bytes 16896 | tf_op jit(solution)/shard_map/scatter-add | solution.py:123
  95.4 14.2 %all-to-all-start.1 = ((f32[16,1,256]{2,1,0:T(1,128)}), f32[16,1,256]{2,1,0:T(1,128)S(1)}, u32[]{:S(2)}, u32[]{:S(2)}) async-start(f32[16,1,256]{2,1,0:T(1,128)} %bitcast.15), calls=%async_computation.1 | async-start | bytes 32768 | tf_op jit(solution)/shard_map/all_to_all | solution.py:33
  111.1 4.2 collective-permute-start
  123.3 4.7 collective-permute-start.2
  129.1 6.2 select_maximum_fusion.4
  136.9 105.7 %while.37 = (s32[]{:T(128)}, f32[8,32,2048]{2,1,0:T(8,128)}, s32[8]{0:T(128)S(1)}, bf16[10,32,18,130]{3,2,1,0:T(8,128)(2,1)}, bf16[32,864]{1,0:T(8,128)(2,1)S(1)...) while((s32[]{:T(128)}, f32[8,32,2048]{2,1,0:T(8,128)}, ...), condition=%wide.region_1.2_spmd, body=%wide.region_0.1_spmd.sunk | while | flops 113246224 | bytes 18012432 | solution.py:81
  141.8 6.1 constant_dynamic-slice_fusion.85
  155.0 6.1 constant_dynamic-slice_fusion.85
  168.4 5.9 constant_dynamic-slice_fusion.85
  181.5 6.0 constant_dynamic-slice_fusion.85
  194.8 6.1 constant_dynamic-slice_fusion.85
  208.1 5.8 constant_dynamic-slice_fusion.85
  221.1 5.8 constant_dynamic-slice_fusion.85
  234.2 6.0 constant_dynamic-slice_fusion.85
  246.6 6.3 copy.120
  253.0 89.0 %scatter_custom_fusion = f32[4096,32]{1,0:T(8,128)} fusion(s32[16384]{0:T(1024)S(1)} %bitcast.888, f32[16384,32]{1,0:T(8,128)} %bitcast.878, f32[]{:T(128)} %constant.165.clone.1), kind=kCustom, calls=%fused_computation.229 | custom fusion | flops 524288 | bytes 524800 | tf_op jit(solution)/shard_map/scatter-add | solution.py:122
  345.0 9.2 %all-to-all-start = ((f32[16,32,256]{2,1,0:T(8,128)}), f32[16,32,256]{2,1,0:T(8,128)S(1)}, u32[]{:S(2)}, u32[]{:S(2)}) async-start(f32[16,32,256]{2,1,0:T(8,128)} %bitcast.14), calls=%async_computation | async-start | bytes 1048576 | tf_op jit(solution)/shard_map/all_to_all | solution.py:33
  354.5 10.6 %all-to-all-done = f32[16,32,256]{2,1,0:T(8,128)S(1)} async-done(((f32[16,32,256]{2,1,0:T(8,128)}), f32[16,32,256]{2,1,0:T(8,128)S(1)}, u32[]{:S(2)}, u32[]{:S(2)}) %all-to-all-start) | async-done | bytes 524320 | tf_op jit(solution)/shard_map/all_to_all | solution.py:33
  369.7 3.9 gather_fusion.1
  373.6 4.6 all-to-all-done.2
  386.9 8.3 %scatter_custom_fusion.3 = f32[4096,256]{1,0:T(8,128)} fusion(s32[1024]{0:T(1024)S(1)} %copy-done.19, f32[1024,256]{1,0:T(8,128)S(1)} %fusion.40, f32[]{:T(128)} %constant.165.clone.1), kind=kCustom, calls=%fused_computation.215 | custom fusion | flops 262144 | bytes 4194308 | tf_op jit(solution)/shard_map/scatter-add | solution.py:148
  395.2 6.9 fusion.5
  408.4 7.1 scatter_custom_fusion.2
  417.4 17.4 %all_gather.3 = f32[32,4096]{1,0:T(8,128)S(1)} all-gather(f32[32,256]{1,0:T(8,128)S(1)} %fusion.32), channel_id=1, replica_groups=mesh['drift'=8,'beam'=16] {'beam'}, dimensions={1}, use_global_device_ids=true | all-gather | bytes 557056 | tf_op jit(solution)/shard_map/all_gather | solution.py:153
  435.4 54.8 %gather_fusion.2 = f32[16384,32]{1,0:T(8,128)} fusion(f32[32,4096]{0,1:T(8,128)S(1)} %copy.113, s32[16384]{0:T(1024)S(1)} %broadcast_clamp_fusion), kind=kCustom, calls=%fused_computation.2 | custom fusion | bytes 4259840 | tf_op jit(solution)/shard_map/jit(_take)/gather | solution.py:155
  490.1 5.2 copy.114
  497.9 10.6 %collective-permute-start.4 = (bf16[1,32,16,128]{3,2,1,0:T(8,128)(2,1)S(1)}, bf16[1,32,16,128]{3,2,1,0:T(8,128)(2,1)S(1)}, u32[]{:S(2)}, u32[]{:S(2)}) collective-permute-start(bf16[1,32,16,128]{3,2,1,0:T(8,128)(2,1)S(1)} %get-tuple-element.356), channel_id=1, source_target_pairs={{0,16},{16,32},{32,48},{48,64},{64,80},{80,96},{96,112},{1,17},{17... | collective-permute-start | bytes 393224 | tf_op jit(solution)/shard_map/ppermute | solution.py:17
  517.8 4.9 collective-permute-start.6
  522.6 113.6 %while.39 = (s32[]{:T(128)}, f32[32,864]{1,0:T(8,128)S(1)}, s32[8]{0:T(128)S(1)}, bf16[8,32,16,128]{3,2,1,0:T(8,128)(2,1)S(1)}, bf16[10,32,18,130]{3,2,1,0:T(8,1...) while((s32[]{:T(128)}, f32[32,864]{1,0:T(8,128)S(1)}, ...), condition=%wide.region_12.13_spmd.clone, body=%wide.region_11.12_spmd.clone.sunk | while | flops 113301520 | bytes 18309432 | solution.py:176
  528.7 6.1 constant_dynamic-slice_fusion.87
  543.0 6.1 constant_dynamic-slice_fusion.87
  557.3 5.9 constant_dynamic-slice_fusion.87
  571.5 6.1 constant_dynamic-slice_fusion.87
  585.7 6.1 constant_dynamic-slice_fusion.87
  600.0 5.8 constant_dynamic-slice_fusion.87
  614.0 5.8 constant_dynamic-slice_fusion.87
  628.1 6.0 constant_dynamic-slice_fusion.87
  639.0 7.1 select_maximum_fusion
  647.6 102.7 %while.38 = (s32[]{:T(128)}, f32[8,32,2048]{2,1,0:T(8,128)}, s32[8]{0:T(128)S(1)}, bf16[10,32,18,130]{3,2,1,0:T(8,128)(2,1)}, bf16[32,864]{1,0:T(8,128)(2,1)S(1)...) while((s32[]{:T(128)}, f32[8,32,2048]{2,1,0:T(8,128)}, ...), condition=%wide.region_10.11_spmd, body=%wide.region_9.10_spmd.sunk | while | flops 113246224 | bytes 18012432 | solution.py:81
  652.0 6.1 constant_dynamic-slice_fusion.86
  664.9 5.9 constant_dynamic-slice_fusion.86
  677.6 6.8 constant_dynamic-slice_fusion.86
  691.3 6.5 constant_dynamic-slice_fusion.86
  704.5 5.9 constant_dynamic-slice_fusion.86
  717.2 5.8 constant_dynamic-slice_fusion.86
  729.8 5.6 constant_dynamic-slice_fusion.86
  742.2 5.8 constant_dynamic-slice_fusion.86
  753.9 23.5 %all-reduce.4.cloned.1.call-done = f32[32,864]{1,0:T(8,128)} async-done(((f32[32,864]{1,0:T(8,128)}), f32[32,864]{1,0:T(8,128)}) %all-reduce.4.cloned.1.call-update) | async-done | bytes 110608 | tf_op jit(solution)/shard_map/psum | solution.py:179
  (825 shorter events, 128.2 us)
Async XLA Ops:
  7.2 378.2 %copy-start = (bf16[256,256]{1,0:T(8,128)(2,1)S(1)}, bf16[256,256]{1,0:T(8,128)(2,1)}, u32[]{:S(2)}) copy-start(bf16[256,256]{1,0:T(8,128)(2,1)} %param.21) | copy-start | bytes 393220
  7.2 110.1 %copy-start.10 = (s32[8,16,128]{2,1,0:T(8,128)S(1)}, s32[8,16,128]{2,1,0:T(8,128)}, u32[]{:S(2)}) copy-start(s32[8,16,128]{2,1,0:T(8,128)} %param.18) | copy-start | bytes 196612
  7.9 120.1 %copy-start.20 = (s32[1024]{0:T(1024)S(1)}, s32[1024]{0:T(1024)}, u32[]{:S(2)}) copy-start(s32[1024]{0:T(1024)} %param.24) | copy-start | bytes 12292
  95.4 249.6 %all-to-all-start.1 = ((f32[16,1,256]{2,1,0:T(1,128)}), f32[16,1,256]{2,1,0:T(1,128)S(1)}, u32[]{:S(2)}, u32[]{:S(2)}) async-start(f32[16,1,256]{2,1,0:T(1,128)} %bitcast.15), calls=%async_computation.1 | async-start | bytes 32768 | tf_op jit(solution)/shard_map/all_to_all | solution.py:33
  111.1 6.8 collective-permute-start
  115.3 6.3 collective-permute-start.1
  122.0 6.7 collective-permute-start.3
  123.3 5.7 collective-permute-start.2
  129.1 7.8 copy-start.5
  242.5 2.1 copy-start.3
  244.6 100.4 %copy-start.2 = (f32[32,8,16,128]{3,2,1,0:T(8,128)}, f32[32,8,16,128]{3,2,1,0:T(8,128)S(1)}, u32[]{:S(2)}) copy-start(f32[32,8,16,128]{3,2,1,0:T(8,128)S(1)} %copy.208) | copy-start | bytes 6291460
  252.9 101.2 %copy-start.13 = (bf16[256,256]{1,0:T(8,128)(2,1)S(1)}, bf16[256,256]{1,0:T(8,128)(2,1)}, u32[]{:S(2)}) copy-start(bf16[256,256]{1,0:T(8,128)(2,1)} %param.25) | copy-start | bytes 393220
  253.0 101.3 %copy-start.15 = (bf16[256,256]{1,0:T(8,128)(2,1)S(1)}, bf16[256,256]{1,0:T(8,128)(2,1)}, u32[]{:S(2)}) copy-start(bf16[256,256]{1,0:T(8,128)(2,1)} %param.22) | copy-start | bytes 393220
  253.0 116.7 %copy-start.19 = (s32[1024]{0:T(1024)S(1)}, s32[1024]{0:T(1024)}, u32[]{:S(2)}) copy-start(s32[1024]{0:T(1024)} %param.23) | copy-start | bytes 12292
  253.0 116.7 %copy-start.21 = (s32[1024]{0:T(1024)S(1)}, s32[1024]{0:T(1024)}, u32[]{:S(2)}) copy-start(s32[1024]{0:T(1024)} %fusion.55) | copy-start | bytes 12292
  345.0 20.1 %all-to-all-start = ((f32[16,32,256]{2,1,0:T(8,128)}), f32[16,32,256]{2,1,0:T(8,128)S(1)}, u32[]{:S(2)}, u32[]{:S(2)}) async-start(f32[16,32,256]{2,1,0:T(8,128)} %bitcast.14), calls=%async_computation | async-start | bytes 1048576 | tf_op jit(solution)/shard_map/all_to_all | solution.py:33
  354.2 24.0 %copy-start.17 = (bf16[32,256]{1,0:T(8,128)(2,1)S(1)}, bf16[32,256]{1,0:T(8,128)(2,1)}, u32[]{:S(2)}) copy-start(bf16[32,256]{1,0:T(8,128)(2,1)} %param.20) | copy-start | bytes 49156
  354.5 15.1 %copy-start.22 = (f32[256]{0:T(256)}, f32[256]{0:T(256)S(1)}, u32[]{:S(2)}) copy-start(f32[256]{0:T(256)S(1)} %broadcast_maximum_fusion) | copy-start | bytes 3076
  365.9 12.3 %all-to-all-start.2 = ((bf16[16,32,256]{2,1,0:T(8,128)(2,1)}), bf16[16,32,256]{2,1,0:T(8,128)(2,1)S(1)}, u32[]{:S(2)}, u32[]{:S(2)}) async-start(bf16[16,32,256]{2,1,0:T(8,128)(2,1)} %broadcast_in_dim.88), calls=%async_computation.2 | async-start | bytes 524288 | tf_op jit(solution)/shard_map/all_to_all | solution.py:39
  395.2 11.7 %copy-start.11 = (s32[16384,1]{0,1:T(1,128)S(1)}, s32[16384,1]{0,1:T(1,128)}, u32[]{:S(2)}) copy-start(s32[16384,1]{0,1:T(1,128)} %compare_select_fusion) | copy-start | bytes 196612
  402.1 6.0 copy-start.18
  402.1 14.9 %copy-start.14 = (bf16[256,256]{1,0:T(8,128)(2,1)S(1)}, bf16[256,256]{1,0:T(8,128)(2,1)}, u32[]{:S(2)}) copy-start(bf16[256,256]{1,0:T(8,128)(2,1)} %param.25) | copy-start | bytes 393220
  402.2 14.9 %copy-start.23 = (f32[256]{0:T(256)S(1)}, f32[256]{0:T(256)}, u32[]{:S(2)}) copy-start(f32[256]{0:T(256)} %copy-done.22) | copy-start | bytes 3076
  403.0 13.9 %all-to-all-start.3 = ((f32[16,32,256]{2,1,0:T(8,128)}), f32[16,32,256]{2,1,0:T(8,128)S(1)}, u32[]{:S(2)}, u32[]{:S(2)}) async-start(f32[16,32,256]{2,1,0:T(8,128)} %bitcast.441), calls=%async_computation.3 | async-start | bytes 1048576 | tf_op jit(solution)/shard_map/all_to_all | solution.py:33
  406.6 370.8 %all-reduce.4.cloned.1.call-start = ((), (), s32[]{:S(2)}) async-start(), calls=%async_computation.4 | async-start | bytes 229376 | tf_op jit(solution)/shard_map/psum | solution.py:179
  408.4 81.7 %copy-start.8 = (f32[256,256]{1,0:T(8,128)}, f32[256,256]{1,0:T(8,128)S(1)}, u32[]{:S(2)}) copy-start(f32[256,256]{1,0:T(8,128)S(1)} %fusion.63) | copy-start | bytes 786436
  495.4 15.1 %copy-start.9 = (f32[256,256]{1,0:T(8,128)S(1)}, f32[256,256]{1,0:T(8,128)}, u32[]{:S(2)}) copy-start(f32[256,256]{1,0:T(8,128)} %copy-done.8) | copy-start | bytes 786436
  495.4 15.1 %copy-start.12 = (f32[256,256]{1,0:T(8,128)S(1)}, f32[256,256]{1,0:T(8,128)}, u32[]{:S(2)}) copy-start(f32[256,256]{1,0:T(8,128)} %scatter_custom_fusion.2) | copy-start | bytes 786436
  495.4 15.1 %copy-start.16 = (bf16[256,256]{1,0:T(8,128)(2,1)S(1)}, bf16[256,256]{1,0:T(8,128)(2,1)}, u32[]{:S(2)}) copy-start(bf16[256,256]{1,0:T(8,128)(2,1)} %param.22) | copy-start | bytes 393220
  497.9 13.4 %collective-permute-start.4 = (bf16[1,32,16,128]{3,2,1,0:T(8,128)(2,1)S(1)}, bf16[1,32,16,128]{3,2,1,0:T(8,128)(2,1)S(1)}, u32[]{:S(2)}, u32[]{:S(2)}) collective-permute-start(bf16[1,32,16,128]{3,2,1,0:T(8,128)(2,1)S(1)} %get-tuple-element.356), channel_id=1, source_target_pairs={{0,16},{16,32},{32,48},{48,64},{64,80},{80,96},{96,112},{1,17},{17... | collective-permute-start | bytes 393224 | tf_op jit(solution)/shard_map/ppermute | solution.py:17
  508.5 6.3 collective-permute-start.5
  511.4 11.3 %copy-start.6 = (bf16[1,32,16,128]{3,2,1,0:T(8,128)(2,1)}, bf16[1,32,16,128]{3,2,1,0:T(8,128)(2,1)S(1)}, u32[]{:S(2)}) copy-start(bf16[1,32,16,128]{3,2,1,0:T(8,128)(2,1)S(1)} %collective-permute-done.4) | copy-start | bytes 393220
  514.8 1.7 copy-start.7
  516.5 120.4 %collective-permute-start.7 = (bf16[10,32,1,128]{3,1,2,0:T(8,128)(2,1)}, bf16[10,32,1,128]{3,1,2,0:T(8,128)(2,1)}, u32[]{:S(2)}, u32[]{:S(2)}) collective-permute-start(bf16[10,32,1,128]{3,1,2,0:T(8,128)(2,1)} %copy.116), channel_id=1, source_target_pairs={{1,0},{2,1},{3,2},{4,3},{5,4},{6,5},{7,6},{8,7},{9,8},{10,9},{11,1... | collective-permute-start | bytes 245768 | tf_op jit(solution)/shard_map/ppermute | solution.py:19
  517.8 120.2 %collective-permute-start.6 = (bf16[10,32,1,128]{3,1,2,0:T(8,128)(2,1)}, bf16[10,32,1,128]{3,1,2,0:T(8,128)(2,1)}, u32[]{:S(2)}, u32[]{:S(2)}) collective-permute-start(bf16[10,32,1,128]{3,1,2,0:T(8,128)(2,1)} %copy.115), channel_id=1, source_target_pairs={{0,1},{1,2},{2,3},{3,4},{4,5},{5,6},{6,7},{7,8},{8,9},{9,10},{10,1... | collective-permute-start | bytes 245768 | tf_op jit(solution)/shard_map/ppermute | solution.py:17
  636.2 0.6 copy-start.4
  750.3 28.7 %copy-start.1 = (bf16[256,256]{1,0:T(8,128)(2,1)S(1)}, bf16[256,256]{1,0:T(8,128)(2,1)}, u32[]{:S(2)}) copy-start(bf16[256,256]{1,0:T(8,128)(2,1)} %param.21) | copy-start | bytes 393220
Sparse Core Ops, SparseCore 0:
  637.0 140.3 all-reduce.3
where the time goes:
time: 792 us; the launch traced here: 786 us
  local copies, waits for them, and re-layouts  271 us (34%)
  other arithmetic  215 us (27%)
  loops' own time  113 us (14%)
  starting transfers between devices  61.7 us (8%)
  waiting for transfers between devices  47.4 us (6%)
  matrix products  45.5 us (6%)
  blocking collectives  17.4 us (2%)
  between operations  15 us (2%)
    dynamic_slice x24, local copies, waits for them, and re-layouts, columns(): piece = lax.dynamic_slice(padded, index, (1, channels, height, depth))  144 us
    scatter-add x1, other arithmetic, body(): sums = jax.ops.segment_sum(by_voxel, frag_ids, num_segments=frag_row).T  89 us
    scatter-add x1, other arithmetic, body(): jax.ops.segment_sum(mask.reshape(-1), frag_ids, num_segments=frag_row)  86.8 us
    another operation x2, loops' own time, convolve(): result = lax.map(one_row, jnp.arange(rows, dtype=jnp.int32))  67.8 us
    gather x2, local copies, waits for them, and re-layouts, body(): jnp.take(mean_all, frag_ids, axis=1).reshape(channels, rows, height, depth)  60 us
    another operation x1, loops' own time, body(): lax.scan(accumulate, jnp.zeros((channels, 27 * channels), f32), jnp.arang...  45.3 us
    all_to_all x3, starting transfers between devices, sum_at_owner(): lax.all_to_all(tiles, axis, split_axis=0, concat_axis=0, tiled=True)  27 us
    ppermute x4, starting transfers between devices, padded_2(): lax.ppermute(tail, axis, [(i, (i + 1) % count) for i in range(ends)])  24.3 us
  transfers between devices with their start and end apart: 13, of which 7 were waited for; matrix products, arithmetic and copies ran while one was open for 45% of the time, Pallas kernels for 0%

commit v1 on v0

v1 whole, which is shorter than its diff:
```python
import functools

import jax
import jax.numpy as jnp
from jax import lax
from jax.experimental import pallas as pl
from jax.experimental.pallas import tpu as pltpu
from jax.sharding import PartitionSpec as P

F32 = jnp.float32
BF16 = jnp.bfloat16
MESH = pl.DeviceIdType.MESH
C = 32
YB = 4
WIN = (YB + 2) * 3 * C
KC = 3 * WIN
NN = (((1,), (0,)), ((), ()))
NT = (((1,), (1,)), ((), ()))
TN = (((0,), (0,)), ((), ()))


def mm(lhs, rhs, dims):
    return lax.dot_general(lhs, rhs, dims, preferred_element_type=F32)


def sig_parts(value):
    sig = 1.0 / (1.0 + jnp.exp(-value))
    return value * sig, sig * (1.0 + value * (1.0 - sig))


def spread(cols, x, row, tile, lane):
    left = jnp.where(lane == 0, 0.0, pltpu.roll(tile, 1, 1)).astype(BF16)
    right = jnp.where(lane == 127, 0.0, pltpu.roll(tile, 127, 1)).astype(BF16)
    mid = tile.astype(BF16)
    for half in range(2):
        for k in range(2):
            inner = row - 8 * half - 4 * k
            if 0 <= inner < YB + 2:
                for tap, part in enumerate((left, mid, right)):
                    start = pl.multiple_of(x * WIN + inner * 96 + tap * C, C)
                    cols[k, pl.ds(start, C), half * 128 : half * 128 + 128] = part


def widen(wide, weight):
    wide[...] = jnp.zeros_like(wide)
    for yo in range(YB):
        for a in range(3):
            at = a * WIN + yo * 96
            wide[yo * C : yo * C + C, at : at + 288] = weight[:, a * 288 : a * 288 + 288]


def kernel(
    nd,
    nb,
    feat,
    occ,
    vf,
    cw,
    cwf,
    emb,
    mw,
    uw,
    es,
    et,
    cot,
    fo,
    gf,
    gc,
    stage,
    plain,
    cols,
    gcols,
    wide,
    gwide,
    lohot,
    ahot,
    slopes,
    bh,
    bc,
    res,
    sums,
    gbig,
    hx,
    hy,
    hc,
    gx,
    gy,
    gcn,
    cs,
    cr,
    ms,
    mr,
    pa,
    ms2,
    mr2,
    bm,
    gs,
    g1,
    g2s,
    g2,
    g3,
    hs,
    hr,
    ks,
    kr,
    ps,
    pr,
):
    d = lax.axis_index("drift")
    b = lax.axis_index("beam")
    dn, dp = lax.rem(d + 1, nd), lax.rem(d + nd - 1, nd)
    bn, bp = lax.rem(b + 1, nb), lax.rem(b + nb - 1, nb)

    barrier = pltpu.get_barrier_semaphore()

    def greet(dev):
        pl.semaphore_signal(barrier, inc=1, device_id=dev, device_id_type=MESH)

    def greet_beam(off, carry):
        greet((d, lax.rem(b + off, nb)))
        return carry

    def greet_drift(off, carry):
        greet((lax.rem(d + off, nd), b))
        return carry

    lax.fori_loop(1, nb, greet_beam, 0)
    lax.fori_loop(1, nd, greet_drift, 0)
    for dev in ((dn, bn), (dn, bp), (dp, bn), (dp, bp)):
        greet(dev)
    pl.semaphore_wait(barrier, nb - 1 + nd - 1 + 4)

    lane = lax.broadcasted_iota(jnp.int32, (C, 128), 1)
    group = lax.broadcasted_iota(jnp.int32, (1, 128), 1) // 8
    occ_f = occ[...].astype(F32)
    rows = []
    for j in range(2):
        row = jnp.zeros((1, 128), F32)
        for q in range(16):
            row = jnp.where(group == q, occ_f[j : j + 1, q : q + 1], row)
        rows.append(row)
    mrow = jnp.concatenate(rows, axis=1)
    x_lo = jnp.where(d > 0, 1.0, 0.0).astype(F32)
    x_hi = jnp.where(d < nd - 1, 1.0, 0.0).astype(F32)
    y_lo = jnp.where(b > 0, 1.0, 0.0).astype(F32)
    y_hi = jnp.where(b < nb - 1, 1.0, 0.0).astype(F32)

    def halo_copies(src, tx, ty, tc, base):
        plan = (
            (src.at[7], tx.at[0], (dn, b)),
            (src.at[0], tx.at[1], (dp, b)),
            (src.at[:, 480:512, :], ty.at[0], (d, bn)),
            (src.at[:, 0:32, :], ty.at[1], (d, bp)),
            (src.at[7, 480:512, :], tc.at[0], (dn, bn)),
            (src.at[7, 0:32, :], tc.at[1], (dn, bp)),
            (src.at[0, 480:512, :], tc.at[2], (dp, bn)),
            (src.at[0, 0:32, :], tc.at[3], (dp, bp)),
        )
        return [
            pltpu.make_async_remote_copy(
                src_ref=s,
                dst_ref=t,
                send_sem=hs.at[base + i],
                recv_sem=hr.at[base + i],
                device_id=dev,
                device_id_type=MESH,
            )
            for i, (s, t, dev) in enumerate(plan)
        ]

    def place_halos(target, tx, ty, tc):
        for y in range(16):
            spread(target, 0, y + 1, tx[0, y * C : y * C + C, :].astype(F32) * x_lo, lane)
            spread(target, 9, y + 1, tx[1, y * C : y * C + C, :].astype(F32) * x_hi, lane)

        def per_x(x, carry):
            spread(target, x + 1, 0, ty[0, x].astype(F32) * y_lo, lane)
            spread(target, x + 1, 17, ty[1, x].astype(F32) * y_hi, lane)
            return carry

        lax.fori_loop(0, 8, per_x, 0)
        spread(target, 0, 0, tc[0].astype(F32) * (x_lo * y_lo), lane)
        spread(target, 0, 17, tc[1].astype(F32) * (x_lo * y_hi), lane)
        spread(target, 9, 0, tc[2].astype(F32) * (x_hi * y_lo), lane)
        spread(target, 9, 17, tc[3].astype(F32) * (x_hi * y_hi), lane)

    def beam_copy(src, dst, base):
        def make(off):
            peer = lax.rem(b + off, nb)
            return pltpu.make_async_remote_copy(
                src_ref=src(peer),
                dst_ref=dst,
                send_sem=ks.at[base, off],
                recv_sem=kr.at[base, off],
                device_id=(d, peer),
                device_id_type=MESH,
            )

        return make

    def drift_copy(src, dst):
        def make(off):
            peer = lax.rem(d + off, nd)
            return pltpu.make_async_remote_copy(
                src_ref=src,
                dst_ref=dst,
                send_sem=ps.at[off],
                recv_sem=pr.at[off],
                device_id=(peer, b),
                device_id_type=MESH,
            )

        return make

    def start_all(make, count):
        def step(off, carry):
            make(off).start()
            return carry

        lax.fori_loop(1, count, step, 0)

    def wait_all(make, count):
        def step(off, carry):
            make(off).wait()
            return carry

        lax.fori_loop(1, count, step, 0)

    def load_row(x, carry):
        stage[...] = feat[x].astype(F32)
        for y in range(16):
            h = y // 8
            tile = stage[pl.ds(y, C, stride=16), :] * mrow[:, h * 128 : h * 128 + 128]
            plain[0, x, y * C : y * C + C, :] = tile.astype(BF16)
            spread(cols, x + 1, y + 1, tile, lane)
        return carry

    lax.fori_loop(0, 8, load_row, 0)
    halos = halo_copies(plain.at[0], hx, hy, hc, 0)
    for copy in halos:
        copy.start()

    sub_lo = lax.broadcasted_iota(jnp.int32, (256, 256), 0)
    sub_hi = lax.broadcasted_iota(jnp.int32, (16, 256), 0)

    def fids(x):
        return jnp.concatenate([vf[x, 0:8, :], vf[x, 8:16, :]], axis=1)

    def counts_of(x, total):
        ids = fids(x)
        for k in range(2):
            parts = []
            for yo in range(YB):
                r = k * YB + yo
                one = ids[r : r + 1, :]
                lo = one & 255
                hi = one >> 8
                lohot[2 * x + k, :, yo * 256 : yo * 256 + 256] = (sub_lo == lo).astype(F32).astype(BF16)
                parts.append(jnp.where(sub_hi == hi, mrow, 0.0).astype(BF16))
            total = total + mm(jnp.concatenate(parts, axis=1), lohot[2 * x + k], NT)
        return total

    counts = lax.fori_loop(0, 8, counts_of, jnp.zeros((16, 256), F32))
    for j in range(16):
        cs[j] = jnp.broadcast_to(counts[j : j + 1, :], (8, 256))
    cr[b] = cs[b]
    count_copies = beam_copy(lambda peer: cs.at[peer], cr.at[b], 0)
    start_all(count_copies, nb)

    widen(wide, cw)
    widen(gwide, cwf)
    for copy in halos:
        copy.wait()
    place_halos(cols, hx, hy, hc)

    sums[...] = jnp.zeros_like(sums)

    def forward(x, carry):
        ids = fids(x)
        for k in range(2):
            g = 2 * x + k
            start = pl.multiple_of(x * WIN, C)
            conv = mm(wide[...], cols[k, pl.ds(start, KC), :], NN)
            silu, slope = sig_parts(conv)
            slopes[g] = slope * mrow
            for yo in range(YB):
                at = pl.multiple_of((x + 1) * WIN + (yo + 1) * 96 + C, C)
                act = cols[k, pl.ds(at, C), :].astype(F32)
                hid = mrow * (act + silu[yo * C : yo * C + C, :])
                r = k * YB + yo
                hi = ids[r : r + 1, :] >> 8
                for q in range(16):
                    ahot[q * C : q * C + C, yo * 256 : yo * 256 + 256] = jnp.where(
                        hi == q, hid, 0.0
                    ).astype(BF16)
            sums[...] += mm(ahot[...], lohot[g], NT)
        return carry

    lax.fori_loop(0, 8, forward, 0)
    for j in range(16):
        ms[j] = sums[j * C : j * C + C, :].astype(BF16)
    mr[b] = ms[b]
    sum_copies = beam_copy(lambda peer: ms.at[peer], mr.at[b], 1)
    start_all(sum_copies, nb)

    sub_e = lax.broadcasted_iota(jnp.int32, (256, 1024), 0)
    src = es[...]
    src_lo = (sub_e == (src & 255)).astype(F32).astype(BF16)
    src_hi = src >> 8
    dst_hot = (sub_e == et[...]).astype(F32).astype(BF16)
    back_agg = mm(cot[...], uw[...], NT).astype(BF16)
    agg_edge = mm(back_agg, dst_hot, TN)

    wait_all(count_copies, nb)
    wait_all(sum_copies, nb)
    total = mr[0].astype(F32)
    number = cr[0]
    for j in range(1, 16):
        total = total + mr[j].astype(F32)
        number = number + cr[j]
    inverse = 1.0 / jnp.maximum(number[0:1, :], 1.0)
    pooled = (total * inverse).astype(BF16)
    pa[b] = pooled
    pool_copies = beam_copy(lambda peer: pa.at[b], pa.at[b], 2)
    start_all(pool_copies, nb)

    pre_own = mm(pooled, emb[...], TN)
    silu_own, slope_own = sig_parts(pre_own)
    own = silu_own.astype(BF16)
    back_self = mm(emb[...], (cot[...].astype(F32) * slope_own).astype(BF16), NT)

    wait_all(pool_copies, nb)
    table = pa[...].reshape(16 * C, 256)
    picked = jnp.zeros((C, 1024), F32)
    every = mm(table, src_lo, NN)
    for q in range(16):
        picked = jnp.where(src_hi == q, every[q * C : q * C + C, :], picked)
    pre_src = mm(emb[...], picked.astype(BF16), TN)
    silu_src, slope_src = sig_parts(pre_src)
    pre_msg = mm(mw[...], silu_src.astype(BF16), TN)
    silu_msg, slope_msg = sig_parts(pre_msg)
    back_pre = (agg_edge * slope_msg).astype(BF16)
    back_src = mm(mw[...], back_pre, NN)
    back_edge = mm(emb[...], (back_src * slope_src).astype(BF16), NN)
    for q in range(16):
        ahot[q * C : q * C + C, :] = jnp.where(src_hi == q, back_edge, 0.0).astype(BF16)
    back_sums = mm(ahot[...], src_lo, NT)
    for j in range(16):
        ms2[j] = back_sums[j * C : j * C + C, :].astype(BF16)
    mr2[b] = ms2[b]
    back_copies = beam_copy(lambda peer: ms2.at[peer], mr2.at[b], 3)
    start_all(back_copies, nb)

    gathered = mm(dst_hot, silu_msg.astype(BF16), NT).astype(BF16)
    fo[...] = (own.astype(F32) + mm(gathered, uw[...], NN)).astype(BF16)

    wait_all(back_copies, nb)
    remote = back_self
    for j in range(16):
        remote = remote + mr2[j].astype(F32)
    bm[b] = (remote * inverse).astype(BF16)
    mean_copies = beam_copy(lambda peer: bm.at[b], bm.at[b], 4)
    start_all(mean_copies, nb)
    wait_all(mean_copies, nb)

    def backward(x, carry):
        ids = fids(x)
        means = bm[...].reshape(16 * C, 256)
        for k in range(2):
            g = 2 * x + k
            for yo in range(YB):
                r = k * YB + yo
                hi = ids[r : r + 1, :] >> 8
                res[...] = mm(means, lohot[g, :, yo * 256 : yo * 256 + 256], NN)
                hid = res[0:C, :]
                for q in range(1, 16):
                    hid = jnp.where(hi == q, res[q * C : q * C + C, :], hid)
                bh[g, yo * C : yo * C + C, :] = hid.astype(BF16)
                back = hid * slopes[g, yo * C : yo * C + C, :]
                bc[g, yo * C : yo * C + C, :] = back.astype(BF16)
                for h in range(2):
                    y = 8 * h + YB * k + yo
                    tile = back[:, h * 128 : h * 128 + 128]
                    plain[1, x, y * C : y * C + C, :] = tile.astype(BF16)
                    spread(gcols, x + 1, y + 1, tile, lane)
        return carry

    lax.fori_loop(0, 8, backward, 0)
    back_halos = halo_copies(plain.at[1], gx, gy, gcn, 8)
    for copy in back_halos:
        copy.start()

    gbig[...] = jnp.zeros_like(gbig)

    def weights(x, carry):
        for k in range(2):
            start = pl.multiple_of(x * WIN, C)
            gbig[...] += mm(bc[2 * x + k], cols[k, pl.ds(start, KC), :], NT)
        return carry

    lax.fori_loop(0, 8, weights, 0)
    gs[...] = jnp.zeros_like(gs)
    for a in range(3):
        part = gbig[0:C, a * WIN : a * WIN + 288]
        for yo in range(1, YB):
            at = a * WIN + yo * 96
            part = part + gbig[yo * C : yo * C + C, at : at + 288]
        gs[:, a * 288 : a * 288 + 288] = part
    for r in range(4):
        for l in range(4):
            g2s[4 * r + l] = gs[r * 8 : r * 8 + 8, l * 256 : l * 256 + 256]
    g1[b] = g2s[b]
    first = beam_copy(lambda peer: g2s.at[peer], g1.at[b], 5)
    start_all(first, nb)

    for copy in back_halos:
        copy.wait()
    place_halos(gcols, gx, gy, gcn)

    def conv_back(x, carry):
        for k in range(2):
            g = 2 * x + k
            start = pl.multiple_of(x * WIN, C)
            conv = mm(gwide[...], gcols[k, pl.ds(start, KC), :], NN)
            full = mrow * (conv + bh[g].astype(F32))
            for yo in range(YB):
                for h in range(2):
                    y = 8 * h + YB * k + yo
                    gf[x, pl.ds(y, C, stride=16), :] = full[
                        yo * C : yo * C + C, h * 128 : h * 128 + 128
                    ]
        return carry

    lax.fori_loop(0, 3, conv_back, 0)
    wait_all(first, nb)
    part = g1[0]
    for j in range(1, 16):
        part = part + g1[j]
    g2[d] = part
    second = drift_copy(g2.at[d], g2.at[d])
    start_all(second, nd)
    lax.fori_loop(3, 6, conv_back, 0)
    wait_all(second, nd)
    part = g2[0]
    for j in range(1, 8):
        part = part + g2[j]
    g3[b] = part
    third = beam_copy(lambda peer: g3.at[b], g3.at[b], 6)
    start_all(third, nb)
    lax.fori_loop(6, 8, conv_back, 0)
    wait_all(third, nb)
    for r in range(4):
        for l in range(4):
            gs[r * 8 : r * 8 + 8, l * 256 : l * 256 + 256] = g3[4 * r + l]
    gc[...] = gs[:, 0:864]


def body(nd, nb, features, occupied, fragments, cw, emb, mw, uw, es, et, cot):
    flipped = cw.reshape(C, 27, C)[:, ::-1, :].transpose(2, 1, 0).reshape(C, 27 * C)
    vmem = pl.BlockSpec(memory_space=pltpu.VMEM)
    scratch = [
        pltpu.VMEM((512, 128), F32),
        pltpu.VMEM((2, 8, 512, 128), BF16),
        pltpu.VMEM((2, 10 * WIN, 256), BF16),
        pltpu.VMEM((2, 10 * WIN, 256), BF16),
        pltpu.VMEM((YB * C, KC), BF16),
        pltpu.VMEM((YB * C, KC), BF16),
        pltpu.VMEM((16, 256, 1024), BF16),
        pltpu.VMEM((512, 1024), BF16),
        pltpu.VMEM((16, YB * C, 256), F32),
        pltpu.VMEM((16, YB * C, 256), BF16),
        pltpu.VMEM((16, YB * C, 256), BF16),
        pltpu.VMEM((512, 256), F32),
        pltpu.VMEM((512, 256), F32),
        pltpu.VMEM((YB * C, KC), F32),
        pltpu.VMEM((2, 512, 128), BF16),
        pltpu.VMEM((2, 8, C, 128), BF16),
        pltpu.VMEM((4, C, 128), BF16),
        pltpu.VMEM((2, 512, 128), BF16),
        pltpu.VMEM((2, 8, C, 128), BF16),
        pltpu.VMEM((4, C, 128), BF16),
        pltpu.VMEM((nb, 8, 256), F32),
        pltpu.VMEM((nb, 8, 256), F32),
        pltpu.VMEM((nb, C, 256), BF16),
        pltpu.VMEM((nb, C, 256), BF16),
        pltpu.VMEM((nb, C, 256), BF16),
        pltpu.VMEM((nb, C, 256), BF16),
        pltpu.VMEM((nb, C, 256), BF16),
        pltpu.VMEM((nb, C, 256), BF16),
        pltpu.VMEM((C, 1024), F32),
        pltpu.VMEM((nb, 8, 256), F32),
        pltpu.VMEM((nb, 8, 256), F32),
        pltpu.VMEM((nd, 8, 256), F32),
        pltpu.VMEM((nb, 8, 256), F32),
        pltpu.SemaphoreType.DMA((16,)),
        pltpu.SemaphoreType.DMA((16,)),
        pltpu.SemaphoreType.DMA((7, nb)),
        pltpu.SemaphoreType.DMA((7, nb)),
        pltpu.SemaphoreType.DMA((nd,)),
        pltpu.SemaphoreType.DMA((nd,)),
    ]
    fo, gf, gc = pl.pallas_call(
        functools.partial(kernel, nd, nb),
        out_shape=(
            jax.ShapeDtypeStruct((256, 256), BF16),
            jax.ShapeDtypeStruct((8, 512, 128), F32),
            jax.ShapeDtypeStruct((C, 27 * C), F32),
        ),
        in_specs=[vmem] * 11,
        out_specs=(vmem, vmem, vmem),
        scratch_shapes=scratch,
        compiler_params=pltpu.CompilerParams(
            collective_id=0, has_side_effects=True, vmem_limit_bytes=60 << 20
        ),
    )(
        features.reshape(8, 512, 128),
        occupied.reshape(2, 16),
        fragments,
        cw,
        flipped,
        emb,
        mw,
        uw,
        es.reshape(1, -1),
        et.reshape(1, -1),
        cot,
    )
    return fo, gf.reshape(8, C, 16, 128), gc


def solution(mesh):
    return jax.shard_map(
        functools.partial(body, mesh.shape["drift"], mesh.shape["beam"]),
        mesh=mesh,
        in_specs=(
            P("drift", None, "beam", None),
            P("drift", "beam", None),
            P("drift", "beam", None),
            P(),
            P(),
            P(),
            P(),
            P(("drift", "beam")),
            P(("drift", "beam")),
            P(("drift", "beam"), None),
        ),
        out_specs=(P(("drift", "beam"), None), P("drift", None, "beam", None), P()),
        check_vma=False,
    )
```

time: 792 us -> 96 us (0.12)
  local copies, waits for them, and re-layouts: 271 us -> 7.95 us
  other arithmetic: 215 us -> 0 us
  loops' own time: 113 us -> 0 us
  Pallas kernels: 0 us -> 87.1 us
  starting transfers between devices: 61.7 us -> 0 us
  waiting for transfers between devices: 47.4 us -> 0 us
  matrix products: 45.5 us -> 0 us
  blocking collectives: 17.4 us -> 0 us
  between operations: 15 us -> 0.66 us
    scatter-add x4 -> x0, other arithmetic: 191 us -> none  [the longest x1 89 us: body(): sums = jax.ops.segment_sum(by_voxel, frag_ids, num_segments=frag_row).T]
    dynamic_slice x48 -> x0, local copies, waits for them, and re-layouts: 158 us -> none  [the longest x24 144 us: columns(): piece = lax.dynamic_slice(padded, index, (1, channels, height, depth))]
    another operation x3 -> x0, loops' own time: 113 us -> none  [the longest x2 67.8 us: convolve(): result = lax.map(one_row, jnp.arange(rows, dtype=jnp.int32))]
    pallas_call x0 -> x1, Pallas kernels: none -> 87.1 us  [body(): pl.pallas_call(functools.partial(kernel, nd, nb), out_shape=(jax.ShapeDty...]
    gather x4 -> x0, local copies, waits for them, and re-layouts: 67.9 us -> none  [the longest x2 60 us: body(): jnp.take(mean_all, frag_ids, axis=1).reshape(channels, rows, height, depth)]
    dot_general x32 -> x0, matrix products: 45.5 us -> none  [the longest x16 22.9 us: one_row(): jnp.dot(weight, columns(padded, row), preferred_element_type=jnp.float32)]
    ppermute x8 -> x0, starting transfers between devices: 30.8 us -> none  [the longest x4 24.3 us: padded_2(): lax.ppermute(tail, axis, [(i, (i + 1) % count) for i in range(ends)])]
    all_to_all x4 -> x0, starting transfers between devices: 30.7 us -> none  [the longest x3 27 us: sum_at_owner(): lax.all_to_all(tiles, axis, split_axis=0, concat_axis=0, tiled=True)]
  transfers between devices with their start and end apart: 13 -> 0, of which waited for: 7 -> 0; matrix products, arithmetic and copies ran while one was open for 45% -> 0% of each run, Pallas kernels for 0% -> 0%
where the time goes in v1:
time: 96 us; the launch traced here: 95.7 us
  Pallas kernels  87.1 us (91%)
  local copies, waits for them, and re-layouts  7.95 us (8%)
    pallas_call x1, Pallas kernels, body(): pl.pallas_call(functools.partial(kernel, nd, nb), out_shape=(jax.ShapeDty...  87.1 us
    unnamed x5, local copies, waits for them, and re-layouts  5.3 us

profile of v1, /device:TPU:1, one launch (start us, length us, event | category | flops | bytes accessed | tf_op | source)
XLA Modules:
  0.0 95.7 jit_solution(15116525275524511796)
XLA Ops:
  0.6 1.0 %reshape.29 = bf16[32,27,32]{2,1,0:T(8,128)(2,1)S(1)} reshape(bf16[32,864]{1,0:T(8,128)(2,1)} %cw.1) | data formatting | bytes 110592 | tf_op jit(solution)/shard_map/reshape | solution.py:459
  1.7 0.2 rev.3
  1.9 0.6 copy.14
  2.4 0.9 reshape.30.cwf
  3.3 87.1 %shard_map.121 = (bf16[256,256]{1,0:T(8,128)(2,1)}, f32[8,512,128]{2,1,0:T(8,128)}, f32[32,864]{1,0:T(8,128)}) custom-call(bf16[8,512,128]{2,1,0:T(8,128)(2,1)} %bitcast.7, s32[2,16]{1,0:T(2,128)} %bitcast.11, s32[8,16,128]{2,1,0:T(8,128)} %vf.1, bf16[32,864]{1,0:T(8,128)(2,1)} %cw.1, bf16[32,864]{1,0:T(8,128)(2,1)} %reshape.30.cwf, bf16[32,256]{1,0:T(8,128)(2,1)} %emb.1, ...), custom_call_target="tpu_custom_call" | custom-call | tf_op jit(solution)/shard_map/pallas_call | solution.py:502
  90.4 1.6 %copy.18 = bf16[256,256]{1,0:T(8,128)(2,1)} copy(bf16[256,256]{1,0:T(8,128)(2,1)} %get-tuple-element.12) | data formatting | bytes 262144
  92.0 0.0 copy-start
  92.0 3.1 %copy.19 = f32[8,32,16,128]{3,2,1,0:T(8,128)} copy(f32[8,32,16,128]{3,2,1,0:T(8,128)} %bitcast.6) | data formatting | bytes 4194304
  95.1 0.0 copy-done
  95.1 0.6 copy.20
Async XLA Ops:
  92.0 3.1 %copy-start = (f32[32,864]{1,0:T(8,128)S(1)}, f32[32,864]{1,0:T(8,128)}, u32[]{:S(2)}) copy-start(f32[32,864]{1,0:T(8,128)} %get-tuple-element.14) | copy-start | bytes 331780

commit v2 on v1

--- a/solution.py
+++ b/solution.py
@@ -38,7 +38,8 @@
             if 0 <= inner < YB + 2:
                 for tap, part in enumerate((left, mid, right)):
                     start = pl.multiple_of(x * WIN + inner * 96 + tap * C, C)
-                    cols[k, pl.ds(start, C), half * 128 : half * 128 + 128] = part
+                    at = k * 256 + half * 128
+                    cols[pl.ds(start, C), at : at + 128] = part
 
 
 def widen(wide, weight):
@@ -46,27 +47,38 @@
     for yo in range(YB):
         for a in range(3):
             at = a * WIN + yo * 96
-            wide[yo * C : yo * C + C, at : at + 288] = weight[:, a * 288 : a * 288 + 288]
+            wide[yo * C : yo * C + C, at : at + 288] = weight[:, a * 288 : a * 288 + 288].astype(BF16)
 
 
 def kernel(
     nd,
     nb,
+    feat_in,
+    occ_in,
+    vf_in,
+    cw_in,
+    emb_in,
+    mw_in,
+    uw_in,
+    es_in,
+    et_in,
+    cot_in,
+    fo,
+    gf,
+    gc,
     feat,
     occ,
     vf,
     cw,
-    cwf,
     emb,
     mw,
     uw,
     es,
     et,
     cot,
-    fo,
-    gf,
-    gc,
+    in_sem,
     stage,
+    flip,
     plain,
     cols,
     gcols,
@@ -74,9 +86,11 @@
     gwide,
     lohot,
     ahot,
+    ahot1,
     slopes,
     bh,
     bc,
+    bc1,
     res,
     sums,
     gbig,
@@ -111,6 +125,25 @@
     dn, dp = lax.rem(d + 1, nd), lax.rem(d + nd - 1, nd)
     bn, bp = lax.rem(b + 1, nb), lax.rem(b + nb - 1, nb)
 
+    loads = [
+        pltpu.make_async_copy(src, dst, in_sem.at[i])
+        for i, (src, dst) in enumerate(
+            (
+                (occ_in, occ),
+                (feat_in, feat),
+                (cw_in, cw),
+                (vf_in, vf),
+                (emb_in, emb),
+                (mw_in, mw),
+                (uw_in, uw),
+                (es_in, es),
+                (et_in, et),
+                (cot_in, cot),
+            )
+        )
+    ]
+    for copy in loads:
+        copy.start()
     barrier = pltpu.get_barrier_semaphore()
 
     def greet(dev):
@@ -128,9 +161,14 @@
     lax.fori_loop(1, nd, greet_drift, 0)
     for dev in ((dn, bn), (dn, bp), (dp, bn), (dp, bp)):
         greet(dev)
-    pl.semaphore_wait(barrier, nb - 1 + nd - 1 + 4)
+    for copy in loads:
+        copy.wait()
 
     lane = lax.broadcasted_iota(jnp.int32, (C, 128), 1)
+    square = (C, C)
+    eye = (
+        lax.broadcasted_iota(jnp.int32, square, 0) == lax.broadcasted_iota(jnp.int32, square, 1)
+    ).astype(F32).astype(BF16)
     group = lax.broadcasted_iota(jnp.int32, (1, 128), 1) // 8
     occ_f = occ[...].astype(F32)
     rows = []
@@ -184,9 +222,12 @@
         spread(target, 9, 0, tc[2].astype(F32) * (x_hi * y_lo), lane)
         spread(target, 9, 17, tc[3].astype(F32) * (x_hi * y_hi), lane)
 
+    by, bz = lax.rem(b, 4), b // 4
+    far = sorted(range(1, 16), key=lambda o: -(min(o % 4, 4 - o % 4) + min(o // 4, 4 - o // 4)))
+
     def beam_copy(src, dst, base):
         def make(off):
-            peer = lax.rem(b + off, nb)
+            peer = 4 * lax.rem(bz + off // 4, 4) + lax.rem(by + off % 4, 4)
             return pltpu.make_async_remote_copy(
                 src_ref=src(peer),
                 dst_ref=dst,
@@ -198,14 +239,14 @@
 
         return make
 
-    def drift_copy(src, dst):
+    def drift_copy(src, dst, base):
         def make(off):
             peer = lax.rem(d + off, nd)
             return pltpu.make_async_remote_copy(
-                src_ref=src,
+                src_ref=src(peer),
                 dst_ref=dst,
-                send_sem=ps.at[off],
-                recv_sem=pr.at[off],
+                send_sem=ps.at[base, off],
+                recv_sem=pr.at[base, off],
                 device_id=(peer, b),
                 device_id_type=MESH,
             )
@@ -213,18 +254,12 @@
         return make
 
     def start_all(make, count):
-        def step(off, carry):
+        for off in far if count == nb else range(1, count):
             make(off).start()
-            return carry
-
-        lax.fori_loop(1, count, step, 0)
 
     def wait_all(make, count):
-        def step(off, carry):
+        for off in range(1, count):
             make(off).wait()
-            return carry
-
-        lax.fori_loop(1, count, step, 0)
 
     def load_row(x, carry):
         stage[...] = feat[x].astype(F32)
@@ -236,12 +271,20 @@
         return carry
 
     lax.fori_loop(0, 8, load_row, 0)
+    widen(wide, cw)
+    turned = mm(cw[...], eye, TN)
+    for t in range(27):
+        flip[:, (26 - t) * C : (27 - t) * C] = turned[t * C : t * C + C, :]
+    widen(gwide, flip)
+    pl.semaphore_wait(barrier, nb - 1 + nd - 1 + 4)
     halos = halo_copies(plain.at[0], hx, hy, hc, 0)
     for copy in halos:
         copy.start()
 
-    sub_lo = lax.broadcasted_iota(jnp.int32, (256, 256), 0)
     sub_hi = lax.broadcasted_iota(jnp.int32, (16, 256), 0)
+    sub_b = sub_hi.astype(F32).astype(BF16)
+    one_b = jnp.ones((16, 256), BF16)
+    zero_b = jnp.zeros((16, 256), BF16)
 
     def fids(x):
         return jnp.concatenate([vf[x, 0:8, :], vf[x, 8:16, :]], axis=1)
@@ -255,7 +298,11 @@
                 one = ids[r : r + 1, :]
                 lo = one & 255
                 hi = one >> 8
-                lohot[2 * x + k, :, yo * 256 : yo * 256 + 256] = (sub_lo == lo).astype(F32).astype(BF16)
+                lo_b = jnp.broadcast_to(lo, (16, 256)).astype(F32).astype(BF16)
+                for j in range(16):
+                    lohot[2 * x + k, j * 16 : j * 16 + 16, yo * 256 : yo * 256 + 256] = jnp.where(
+                        sub_b == lo_b - BF16(16 * j), one_b, zero_b
+                    )
                 parts.append(jnp.where(sub_hi == hi, mrow, 0.0).astype(BF16))
             total = total + mm(jnp.concatenate(parts, axis=1), lohot[2 * x + k], NT)
         return total
@@ -267,41 +314,58 @@
     count_copies = beam_copy(lambda peer: cs.at[peer], cr.at[b], 0)
     start_all(count_copies, nb)
 
-    widen(wide, cw)
-    widen(gwide, cwf)
     for copy in halos:
         copy.wait()
     place_halos(cols, hx, hy, hc)
 
     sums[...] = jnp.zeros_like(sums)
 
+    zero_h = jnp.zeros((C, 256), BF16)
+
+    def convolve(x, k, hot):
+        ids = fids(x)
+        start = pl.multiple_of(x * WIN, C)
+        conv = mm(wide[...], cols[pl.ds(start, KC), k * 256 : k * 256 + 256], NN)
+        slopes[2 * x + k] = conv
+        silu = conv / (1.0 + jnp.exp(-conv))
+        for yo in range(YB):
+            at = pl.multiple_of((x + 1) * WIN + (yo + 1) * 96 + C, C)
+            act = cols[pl.ds(at, C), k * 256 : k * 256 + 256].astype(F32)
+            hid = (mrow * (act + silu[yo * C : yo * C + C, :])).astype(BF16)
+            r = k * YB + yo
+            hi = jnp.broadcast_to(ids[r : r + 1, :] >> 8, (C, 256)).astype(F32).astype(BF16)
+            for q in range(16):
+                hot[q * C : q * C + C, yo * 256 : yo * 256 + 256] = jnp.where(
+                    hi == BF16(q), hid, zero_h
+                )
+
+    def scatter(g, hot):
+        sums[...] += mm(hot[...], lohot[g], NT)
+
     def forward(x, carry):
-        ids = fids(x)
-        for k in range(2):
-            g = 2 * x + k
-            start = pl.multiple_of(x * WIN, C)
-            conv = mm(wide[...], cols[k, pl.ds(start, KC), :], NN)
-            silu, slope = sig_parts(conv)
-            slopes[g] = slope * mrow
-            for yo in range(YB):
-                at = pl.multiple_of((x + 1) * WIN + (yo + 1) * 96 + C, C)
-                act = cols[k, pl.ds(at, C), :].astype(F32)
-                hid = mrow * (act + silu[yo * C : yo * C + C, :])
-                r = k * YB + yo
-                hi = ids[r : r + 1, :] >> 8
-                for q in range(16):
-                    ahot[q * C : q * C + C, yo * 256 : yo * 256 + 256] = jnp.where(
-                        hi == q, hid, 0.0
-                    ).astype(BF16)
-            sums[...] += mm(ahot[...], lohot[g], NT)
+        scatter(2 * x, ahot)
+        convolve(x, 1, ahot1)
+        scatter(2 * x + 1, ahot1)
+        convolve(x + 1, 0, ahot)
         return carry
 
-    lax.fori_loop(0, 8, forward, 0)
+    convolve(0, 0, ahot)
+    lax.fori_loop(0, 7, forward, 0)
+    scatter(14, ahot)
+    convolve(7, 1, ahot1)
+    scatter(15, ahot1)
     for j in range(16):
         ms[j] = sums[j * C : j * C + C, :].astype(BF16)
     mr[b] = ms[b]
     sum_copies = beam_copy(lambda peer: ms.at[peer], mr.at[b], 1)
     start_all(sum_copies, nb)
+
+    def slope_of(g, carry):
+        sig = 1.0 / (1.0 + jnp.exp(-slopes[g]))
+        slopes[g] = mrow * (sig * (1.0 + slopes[g] * (1.0 - sig)))
+        return carry
+
+    lax.fori_loop(0, 16, slope_of, 0)
 
     sub_e = lax.broadcasted_iota(jnp.int32, (256, 1024), 0)
     src = es[...]
@@ -363,7 +427,7 @@
     start_all(mean_copies, nb)
     wait_all(mean_copies, nb)
 
-    def backward(x, carry):
+    def spread_means(x, out):
         ids = fids(x)
         means = bm[...].reshape(16 * C, 256)
         for k in range(2):
@@ -377,28 +441,34 @@
                     hid = jnp.where(hi == q, res[q * C : q * C + C, :], hid)
                 bh[g, yo * C : yo * C + C, :] = hid.astype(BF16)
                 back = hid * slopes[g, yo * C : yo * C + C, :]
-                bc[g, yo * C : yo * C + C, :] = back.astype(BF16)
+                out[yo * C : yo * C + C, k * 256 : k * 256 + 256] = back.astype(BF16)
                 for h in range(2):
                     y = 8 * h + YB * k + yo
                     tile = back[:, h * 128 : h * 128 + 128]
                     plain[1, x, y * C : y * C + C, :] = tile.astype(BF16)
                     spread(gcols, x + 1, y + 1, tile, lane)
+
+    gbig[...] = jnp.zeros_like(gbig)
+
+    def weights(x, back):
+        start = pl.multiple_of(x * WIN, C)
+        gbig[...] += mm(back[...], cols[pl.ds(start, KC), :], NT)
+
+    def backward(i, carry):
+        weights(2 * i, bc)
+        spread_means(2 * i + 1, bc1)
+        weights(2 * i + 1, bc1)
+        spread_means(2 * i + 2, bc)
         return carry
 
-    lax.fori_loop(0, 8, backward, 0)
+    spread_means(0, bc)
+    lax.fori_loop(0, 3, backward, 0)
+    weights(6, bc)
+    spread_means(7, bc1)
     back_halos = halo_copies(plain.at[1], gx, gy, gcn, 8)
     for copy in back_halos:
         copy.start()
-
-    gbig[...] = jnp.zeros_like(gbig)
-
-    def weights(x, carry):
-        for k in range(2):
-            start = pl.multiple_of(x * WIN, C)
-            gbig[...] += mm(bc[2 * x + k], cols[k, pl.ds(start, KC), :], NT)
-        return carry
-
-    lax.fori_loop(0, 8, weights, 0)
+    weights(7, bc1)
     gs[...] = jnp.zeros_like(gs)
     for a in range(3):
         part = gbig[0:C, a * WIN : a * WIN + 288]
@@ -406,22 +476,18 @@
             at = a * WIN + yo * 96
             part = part + gbig[yo * C : yo * C + C, at : at + 288]
         gs[:, a * 288 : a * 288 + 288] = part
-    for r in range(4):
+    for r in range(2):
         for l in range(4):
-            g2s[4 * r + l] = gs[r * 8 : r * 8 + 8, l * 256 : l * 256 + 256]
-    g1[b] = g2s[b]
-    first = beam_copy(lambda peer: g2s.at[peer], g1.at[b], 5)
-    start_all(first, nb)
-
-    for copy in back_halos:
-        copy.wait()
-    place_halos(gcols, gx, gy, gcn)
+            g2s[4 * r + l] = gs[r * 16 : r * 16 + 16, l * 256 : l * 256 + 256]
+    g1[d] = g2s[d]
+    first = drift_copy(lambda peer: g2s.at[peer], g1.at[d], 0)
+    start_all(first, nd)
 
     def conv_back(x, carry):
         for k in range(2):
             g = 2 * x + k
             start = pl.multiple_of(x * WIN, C)
-            conv = mm(gwide[...], gcols[k, pl.ds(start, KC), :], NN)
+            conv = mm(gwide[...], gcols[pl.ds(start, KC), k * 256 : k * 256 + 256], NN)
             full = mrow * (conv + bh[g].astype(F32))
             for yo in range(YB):
                 for h in range(2):
@@ -431,45 +497,74 @@
                     ]
         return carry
 
+    wait_all(first, nd)
+    part = g1[0]
+    for j in range(1, 8):
+        part = part + g1[j]
+    g2[b] = part.astype(BF16)
+    second = beam_copy(lambda peer: g2.at[b], g2.at[b], 5)
+    start_all(second, nb)
+    for copy in back_halos:
+        copy.wait()
+    place_halos(gcols, gx, gy, gcn)
     lax.fori_loop(0, 3, conv_back, 0)
-    wait_all(first, nb)
-    part = g1[0]
+    wait_all(second, nb)
+    part = g2[0].astype(F32)
     for j in range(1, 16):
-        part = part + g1[j]
-    g2[d] = part
-    second = drift_copy(g2.at[d], g2.at[d])
-    start_all(second, nd)
-    lax.fori_loop(3, 6, conv_back, 0)
-    wait_all(second, nd)
-    part = g2[0]
-    for j in range(1, 8):
-        part = part + g2[j]
-    g3[b] = part
-    third = beam_copy(lambda peer: g3.at[b], g3.at[b], 6)
-    start_all(third, nb)
-    lax.fori_loop(6, 8, conv_back, 0)
-    wait_all(third, nb)
-    for r in range(4):
+        part = part + g2[j].astype(F32)
+    g3[d] = part
+    third = drift_copy(lambda peer: g3.at[d], g3.at[d], 1)
+    start_all(third, nd)
+    lax.fori_loop(3, 8, conv_back, 0)
+    wait_all(third, nd)
+    for r in range(2):
         for l in range(4):
-            gs[r * 8 : r * 8 + 8, l * 256 : l * 256 + 256] = g3[4 * r + l]
+            gs[r * 16 : r * 16 + 16, l * 256 : l * 256 + 256] = g3[4 * r + l]
     gc[...] = gs[:, 0:864]
 
 
+def store(fo, gf, gc, fo_out, gf_out, gc_out, sem):
+    copies = [
+        pltpu.make_async_copy(src, dst, sem.at[i])
+        for i, (src, dst) in enumerate(((gf, gf_out), (fo, fo_out), (gc, gc_out)))
+    ]
+    for copy in copies:
+        copy.start()
+    for copy in copies:
+        copy.wait()
+
+
 def body(nd, nb, features, occupied, fragments, cw, emb, mw, uw, es, et, cot):
-    flipped = cw.reshape(C, 27, C)[:, ::-1, :].transpose(2, 1, 0).reshape(C, 27 * C)
     vmem = pl.BlockSpec(memory_space=pltpu.VMEM)
-    scratch = [
+    hbm = pl.BlockSpec(memory_space=pltpu.HBM)
+    inputs = (
+        features.reshape(8, 512, 128),
+        occupied.reshape(2, 16),
+        fragments,
+        cw,
+        emb,
+        mw,
+        uw,
+        es.reshape(1, -1),
+        et.reshape(1, -1),
+        cot,
+    )
+    scratch = [pltpu.VMEM(one.shape, one.dtype) for one in inputs] + [
+        pltpu.SemaphoreType.DMA((10,)),
         pltpu.VMEM((512, 128), F32),
+        pltpu.VMEM((C, 27 * C), F32),
         pltpu.VMEM((2, 8, 512, 128), BF16),
-        pltpu.VMEM((2, 10 * WIN, 256), BF16),
-        pltpu.VMEM((2, 10 * WIN, 256), BF16),
+        pltpu.VMEM((10 * WIN, 512), BF16),
+        pltpu.VMEM((10 * WIN, 512), BF16),
         pltpu.VMEM((YB * C, KC), BF16),
         pltpu.VMEM((YB * C, KC), BF16),
         pltpu.VMEM((16, 256, 1024), BF16),
         pltpu.VMEM((512, 1024), BF16),
+        pltpu.VMEM((512, 1024), BF16),
         pltpu.VMEM((16, YB * C, 256), F32),
         pltpu.VMEM((16, YB * C, 256), BF16),
-        pltpu.VMEM((16, YB * C, 256), BF16),
+        pltpu.VMEM((YB * C, 512), BF16),
+        pltpu.VMEM((YB * C, 512), BF16),
         pltpu.VMEM((512, 256), F32),
         pltpu.VMEM((512, 256), F32),
         pltpu.VMEM((YB * C, KC), F32),
@@ -488,43 +583,39 @@
         pltpu.VMEM((nb, C, 256), BF16),
         pltpu.VMEM((nb, C, 256), BF16),
         pltpu.VMEM((C, 1024), F32),
-        pltpu.VMEM((nb, 8, 256), F32),
-        pltpu.VMEM((nb, 8, 256), F32),
-        pltpu.VMEM((nd, 8, 256), F32),
-        pltpu.VMEM((nb, 8, 256), F32),
+        pltpu.VMEM((nd, 16, 256), F32),
+        pltpu.VMEM((nd, 16, 256), F32),
+        pltpu.VMEM((nb, 16, 256), BF16),
+        pltpu.VMEM((nd, 16, 256), F32),
         pltpu.SemaphoreType.DMA((16,)),
         pltpu.SemaphoreType.DMA((16,)),
-        pltpu.SemaphoreType.DMA((7, nb)),
-        pltpu.SemaphoreType.DMA((7, nb)),
-        pltpu.SemaphoreType.DMA((nd,)),
-        pltpu.SemaphoreType.DMA((nd,)),
+        pltpu.SemaphoreType.DMA((6, nb)),
+        pltpu.SemaphoreType.DMA((6, nb)),
+        pltpu.SemaphoreType.DMA((2, nd)),
+        pltpu.SemaphoreType.DMA((2, nd)),
     ]
-    fo, gf, gc = pl.pallas_call(
+    results = pl.pallas_call(
         functools.partial(kernel, nd, nb),
         out_shape=(
-            jax.ShapeDtypeStruct((256, 256), BF16),
-            jax.ShapeDtypeStruct((8, 512, 128), F32),
-            jax.ShapeDtypeStruct((C, 27 * C), F32),
+            pltpu.VMEM((256, 256), BF16),
+            pltpu.VMEM((8, 512, 128), F32),
+            pltpu.VMEM((C, 27 * C), F32),
         ),
-        in_specs=[vmem] * 11,
+        in_specs=[hbm] * 10,
         out_specs=(vmem, vmem, vmem),
         scratch_shapes=scratch,
         compiler_params=pltpu.CompilerParams(
-            collective_id=0, has_side_effects=True, vmem_limit_bytes=60 << 20
+            collective_id=0, has_side_effects=True, vmem_limit_bytes=44 << 20
         ),
-    )(
-        features.reshape(8, 512, 128),
-        occupied.reshape(2, 16),
-        fragments,
-        cw,
-        flipped,
-        emb,
-        mw,
-        uw,
-        es.reshape(1, -1),
-        et.reshape(1, -1),
-        cot,
-    )
+    )(*[pltpu.with_memory_space_constraint(one, pltpu.HBM) for one in inputs])
+    fo, gf, gc = pl.pallas_call(
+        store,
+        out_shape=tuple(jax.ShapeDtypeStruct(one.shape, one.dtype) for one in results),
+        in_specs=[vmem] * 3,
+        out_specs=(hbm,) * 3,
+        scratch_shapes=[pltpu.SemaphoreType.DMA((3,))],
+        compiler_params=pltpu.CompilerParams(vmem_limit_bytes=1 << 20),
+    )(*results)
     return fo, gf.reshape(8, C, 16, 128), gc
 
 

time: 96 us -> 81.5 us (0.85)
  local copies, waits for them, and re-layouts: 7.95 us -> 0 us
  Pallas kernels: 87.1 us -> 80.7 us
    pallas_call x1 -> x2, Pallas kernels: 87.1 us -> 80.7 us  [the longest x1 79.3 us: body(): pl.pallas_call(functools.partial(kernel, nd, nb), out_shape=(pltpu.VMEM((...]
    unnamed x5 -> x0, local copies, waits for them, and re-layouts: 5.3 us -> none
    reshape x2 -> x0, local copies, waits for them, and re-layouts: 1.9 us -> none  [body(): cw.reshape(C, 27, C)[:, ::-1, :].transpose(2, 1, 0).reshape(C, 27 * C)]
where the time goes in v2:
time: 81.5 us; the launch traced here: 81.3 us
  Pallas kernels  80.7 us (99%)
    pallas_call x1, Pallas kernels, body(): pl.pallas_call(functools.partial(kernel, nd, nb), out_shape=(pltpu.VMEM((...  79.3 us

profile of v2, /device:TPU:1, one launch (start us, length us, event | category | flops | bytes accessed | tf_op | source)
XLA Modules:
  0.0 81.3 jit_solution(17640743387367025289)
XLA Ops:
  0.6 79.3 %shard_map.121 = (bf16[256,256]{1,0:T(8,128)(2,1)S(1)}, f32[8,512,128]{2,1,0:T(8,128)S(1)}, f32[32,864]{1,0:T(8,128)S(1)}) custom-call(bf16[8,512,128]{2,1,0:T(8,128)(2,1)} %bitcast.5, s32[2,16]{1,0:T(2,128)} %bitcast.8, s32[8,16,128]{2,1,0:T(8,128)} %vf_in.1, bf16[32,864]{1,0:T(8,128)(2,1)} %cw_in.1, bf16[32,256]{1,0:T(8,128)(2,1)} %emb_in.1, ...), custom_call_target="tpu_custom_call" | custom-call | tf_op jit(solution)/shard_map/pallas_call | solution.py:597
  79.9 1.4 %shard_map.122 = (bf16[256,256]{1,0:T(8,128)(2,1)}, f32[8,512,128]{2,1,0:T(8,128)}, f32[32,864]{1,0:T(8,128)}) custom-call(bf16[256,256]{1,0:T(8,128)(2,1)S(1)} %get-tuple-element.9.fo, f32[8,512,128]{2,1,0:T(8,128)S(1)} %get-tuple-element.10.gf, f32[32,864]{1,0:T(8,128)S(1)} %get-tuple-element.11.gc), custom_call_target="tpu_custom_call" | custom-call | tf_op jit(solution)/shard_map/pallas_call | solution.py:611

commit v3 on v2

--- a/solution.py
+++ b/solution.py
@@ -14,6 +14,7 @@
 YB = 4
 WIN = (YB + 2) * 3 * C
 KC = 3 * WIN
+NEAR = 11
 NN = (((1,), (0,)), ((), ()))
 NT = (((1,), (1,)), ((), ()))
 TN = (((0,), (0,)), ((), ()))
@@ -142,8 +143,6 @@
             )
         )
     ]
-    for copy in loads:
-        copy.start()
     barrier = pltpu.get_barrier_semaphore()
 
     def greet(dev):
@@ -161,6 +160,8 @@
     lax.fori_loop(1, nd, greet_drift, 0)
     for dev in ((dn, bn), (dn, bp), (dp, bn), (dp, bp)):
         greet(dev)
+    for copy in loads:
+        copy.start()
     for copy in loads:
         copy.wait()
 
@@ -185,14 +186,14 @@
 
     def halo_copies(src, tx, ty, tc, base):
         plan = (
-            (src.at[7], tx.at[0], (dn, b)),
-            (src.at[0], tx.at[1], (dp, b)),
-            (src.at[:, 480:512, :], ty.at[0], (d, bn)),
-            (src.at[:, 0:32, :], ty.at[1], (d, bp)),
             (src.at[7, 480:512, :], tc.at[0], (dn, bn)),
             (src.at[7, 0:32, :], tc.at[1], (dn, bp)),
             (src.at[0, 480:512, :], tc.at[2], (dp, bn)),
             (src.at[0, 0:32, :], tc.at[3], (dp, bp)),
+            (src.at[:, 480:512, :], ty.at[0], (d, bn)),
+            (src.at[:, 0:32, :], ty.at[1], (d, bp)),
+            (src.at[7], tx.at[0], (dn, b)),
+            (src.at[0], tx.at[1], (dp, b)),
         )
         return [
             pltpu.make_async_remote_copy(
@@ -223,14 +224,16 @@
         spread(target, 9, 17, tc[3].astype(F32) * (x_hi * y_hi), lane)
 
     by, bz = lax.rem(b, 4), b // 4
-    far = sorted(range(1, 16), key=lambda o: -(min(o % 4, 4 - o % 4) + min(o // 4, 4 - o // 4)))
+    near = sorted(range(16), key=lambda o: min(o % 4, 4 - o % 4) + min(o // 4, 4 - o // 4))
+    far = near[:0:-1]
+    owner = [4 * lax.rem(bz + 4 - o // 4, 4) + lax.rem(by + 4 - o % 4, 4) for o in near]
 
     def beam_copy(src, dst, base):
         def make(off):
             peer = 4 * lax.rem(bz + off // 4, 4) + lax.rem(by + off % 4, 4)
             return pltpu.make_async_remote_copy(
                 src_ref=src(peer),
-                dst_ref=dst,
+                dst_ref=dst(off) if callable(dst) else dst,
                 send_sem=ks.at[base, off],
                 recv_sem=kr.at[base, off],
                 device_id=(d, peer),
@@ -271,11 +274,6 @@
         return carry
 
     lax.fori_loop(0, 8, load_row, 0)
-    widen(wide, cw)
-    turned = mm(cw[...], eye, TN)
-    for t in range(27):
-        flip[:, (26 - t) * C : (27 - t) * C] = turned[t * C : t * C + C, :]
-    widen(gwide, flip)
     pl.semaphore_wait(barrier, nb - 1 + nd - 1 + 4)
     halos = halo_copies(plain.at[0], hx, hy, hc, 0)
     for copy in halos:
@@ -314,6 +312,11 @@
     count_copies = beam_copy(lambda peer: cs.at[peer], cr.at[b], 0)
     start_all(count_copies, nb)
 
+    widen(wide, cw)
+    turned = mm(cw[...], eye, TN)
+    for t in range(27):
+        flip[:, (26 - t) * C : (27 - t) * C] = turned[t * C : t * C + C, :]
+    widen(gwide, flip)
     for copy in halos:
         copy.wait()
     place_halos(cols, hx, hy, hc)
@@ -422,63 +425,92 @@
     remote = back_self
     for j in range(16):
         remote = remote + mr2[j].astype(F32)
-    bm[b] = (remote * inverse).astype(BF16)
-    mean_copies = beam_copy(lambda peer: bm.at[b], bm.at[b], 4)
+    bm[0] = (remote * inverse).astype(BF16)
+    mean_copies = beam_copy(lambda peer: bm.at[0], lambda off: bm.at[near.index(off)], 4)
     start_all(mean_copies, nb)
-    wait_all(mean_copies, nb)
-
-    def spread_means(x, out):
+    gbig[...] = jnp.zeros_like(gbig)
+    for off in near[1:NEAR]:
+        mean_copies(off).wait()
+
+    def gather_near(x, carry):
         ids = fids(x)
-        means = bm[...].reshape(16 * C, 256)
+        means = bm[0:NEAR].reshape(NEAR * C, 256)
         for k in range(2):
-            g = 2 * x + k
             for yo in range(YB):
                 r = k * YB + yo
                 hi = ids[r : r + 1, :] >> 8
-                res[...] = mm(means, lohot[g, :, yo * 256 : yo * 256 + 256], NN)
+                res[0 : NEAR * C, :] = mm(means, lohot[2 * x + k, :, yo * 256 : yo * 256 + 256], NN)
                 hid = res[0:C, :]
-                for q in range(1, 16):
-                    hid = jnp.where(hi == q, res[q * C : q * C + C, :], hid)
-                bh[g, yo * C : yo * C + C, :] = hid.astype(BF16)
-                back = hid * slopes[g, yo * C : yo * C + C, :]
-                out[yo * C : yo * C + C, k * 256 : k * 256 + 256] = back.astype(BF16)
-                for h in range(2):
-                    y = 8 * h + YB * k + yo
-                    tile = back[:, h * 128 : h * 128 + 128]
-                    plain[1, x, y * C : y * C + C, :] = tile.astype(BF16)
-                    spread(gcols, x + 1, y + 1, tile, lane)
-
-    gbig[...] = jnp.zeros_like(gbig)
-
-    def weights(x, back):
-        start = pl.multiple_of(x * WIN, C)
-        gbig[...] += mm(back[...], cols[pl.ds(start, KC), :], NT)
+                for q in range(1, NEAR):
+                    hid = jnp.where(hi == owner[q], res[q * C : q * C + C, :], hid)
+                bh[2 * x + k, yo * C : yo * C + C, :] = hid.astype(BF16)
+        return carry
+
+    lax.fori_loop(0, 8, gather_near, 0)
+    for off in near[NEAR:]:
+        mean_copies(off).wait()
+
+    def gather_far(i, out):
+        means = bm[NEAR:16].reshape((16 - NEAR) * C, 256)
+        for j in range(2):
+            x = 2 * i + j
+            ids = fids(x)
+            for k in range(2):
+                g = 2 * x + k
+                for yo in range(YB):
+                    r = k * YB + yo
+                    hi = ids[r : r + 1, :] >> 8
+                    got = mm(means, lohot[g, :, yo * 256 : yo * 256 + 256], NN)
+                    hid = bh[g, yo * C : yo * C + C, :].astype(F32)
+                    for q in range(NEAR, 16):
+                        at = (q - NEAR) * C
+                        hid = jnp.where(hi == owner[q], got[at : at + C, :], hid)
+                    bh[g, yo * C : yo * C + C, :] = hid.astype(BF16)
+                    back = hid * slopes[g, yo * C : yo * C + C, :]
+                    row = j * YB * C + yo * C
+                    out[row : row + C, k * 256 : k * 256 + 256] = back.astype(BF16)
+                    for h in range(2):
+                        y = 8 * h + YB * k + yo
+                        tile = back[:, h * 128 : h * 128 + 128]
+                        plain[1, x, y * C : y * C + C, :] = tile.astype(BF16)
+                        spread(gcols, x + 1, y + 1, tile, lane)
+
+    def weights(i, back):
+        start = pl.multiple_of(2 * i * WIN, C)
+        gbig[...] += mm(cols[pl.ds(start, 4 * WIN), :], back[...], NT)
 
     def backward(i, carry):
-        weights(2 * i, bc)
-        spread_means(2 * i + 1, bc1)
-        weights(2 * i + 1, bc1)
-        spread_means(2 * i + 2, bc)
-        return carry
-
-    spread_means(0, bc)
+        weights(i, bc)
+        gather_far(i + 1, bc1)
+        bc[...] = bc1[...]
+        return carry
+
+    gather_far(0, bc)
     lax.fori_loop(0, 3, backward, 0)
-    weights(6, bc)
-    spread_means(7, bc1)
     back_halos = halo_copies(plain.at[1], gx, gy, gcn, 8)
     for copy in back_halos:
         copy.start()
-    weights(7, bc1)
-    gs[...] = jnp.zeros_like(gs)
+    weights(3, bc)
+    quarter = lax.broadcasted_iota(jnp.int32, (288, 128), 1) // C
     for a in range(3):
-        part = gbig[0:C, a * WIN : a * WIN + 288]
-        for yo in range(1, YB):
-            at = a * WIN + yo * 96
-            part = part + gbig[yo * C : yo * C + C, at : at + 288]
-        gs[:, a * 288 : a * 288 + 288] = part
-    for r in range(2):
-        for l in range(4):
-            g2s[4 * r + l] = gs[r * 16 : r * 16 + 16, l * 256 : l * 256 + 256]
+        total = None
+        for j in range(2):
+            at = (j + a) * WIN
+            part = gbig[at : at + 288, j * 128 : j * 128 + 128]
+            for yo in range(1, YB):
+                down = at + yo * 96
+                part = jnp.where(
+                    quarter == yo, gbig[down : down + 288, j * 128 : j * 128 + 128], part
+                )
+            total = part if total is None else total + part
+        total = total + pltpu.roll(total, 64, 1)
+        gs[a * 288 : a * 288 + 288, :] = total + pltpu.roll(total, 32, 1)
+    packed = gs[0:216, :]
+    for j in range(1, 4):
+        packed = jnp.where(quarter[0:216] == j, gs[j * 216 : j * 216 + 216, :], packed)
+    turned = jnp.concatenate([packed, jnp.zeros((40, 128), F32)], axis=0).T
+    for j in range(8):
+        g2s[j] = turned[j * 16 : j * 16 + 16, :]
     g1[d] = g2s[d]
     first = drift_copy(lambda peer: g2s.at[peer], g1.at[d], 0)
     start_all(first, nd)
@@ -517,10 +549,9 @@
     start_all(third, nd)
     lax.fori_loop(3, 8, conv_back, 0)
     wait_all(third, nd)
-    for r in range(2):
-        for l in range(4):
-            gs[r * 16 : r * 16 + 16, l * 256 : l * 256 + 256] = g3[4 * r + l]
-    gc[...] = gs[:, 0:864]
+    for j in range(8):
+        at = (j // 2) * 216
+        gc[(j % 2) * 16 : (j % 2) * 16 + 16, at : at + 216] = g3[j, :, 0:216]
 
 
 def store(fo, gf, gc, fo_out, gf_out, gc_out, sem):
@@ -563,11 +594,11 @@
         pltpu.VMEM((512, 1024), BF16),
         pltpu.VMEM((16, YB * C, 256), F32),
         pltpu.VMEM((16, YB * C, 256), BF16),
-        pltpu.VMEM((YB * C, 512), BF16),
-        pltpu.VMEM((YB * C, 512), BF16),
+        pltpu.VMEM((2 * YB * C, 512), BF16),
+        pltpu.VMEM((2 * YB * C, 512), BF16),
         pltpu.VMEM((512, 256), F32),
         pltpu.VMEM((512, 256), F32),
-        pltpu.VMEM((YB * C, KC), F32),
+        pltpu.VMEM((4 * WIN, 256), F32),
         pltpu.VMEM((2, 512, 128), BF16),
         pltpu.VMEM((2, 8, C, 128), BF16),
         pltpu.VMEM((4, C, 128), BF16),
@@ -582,7 +613,7 @@
         pltpu.VMEM((nb, C, 256), BF16),
         pltpu.VMEM((nb, C, 256), BF16),
         pltpu.VMEM((nb, C, 256), BF16),
-        pltpu.VMEM((C, 1024), F32),
+        pltpu.VMEM((27 * C, 128), F32),
         pltpu.VMEM((nd, 16, 256), F32),
         pltpu.VMEM((nd, 16, 256), F32),
         pltpu.VMEM((nb, 16, 256), BF16),
@@ -605,7 +636,7 @@
         out_specs=(vmem, vmem, vmem),
         scratch_shapes=scratch,
         compiler_params=pltpu.CompilerParams(
-            collective_id=0, has_side_effects=True, vmem_limit_bytes=44 << 20
+            collective_id=0, has_side_effects=True, vmem_limit_bytes=48 << 20
         ),
     )(*[pltpu.with_memory_space_constraint(one, pltpu.HBM) for one in inputs])
     fo, gf, gc = pl.pallas_call(

time: 81.5 us -> 78.3 us (0.961)
  Pallas kernels: 80.7 us -> 77.5 us
    pallas_call x1, Pallas kernels: 79.3 us -> 76.1 us  [body(): pl.pallas_call(functools.partial(kernel, nd, nb), out_shape=(pltpu.VMEM((...]
where the time goes in v3:
time: 78.3 us; the launch traced here: 78.2 us
  Pallas kernels  77.5 us (99%)
    pallas_call x1, Pallas kernels, body(): pl.pallas_call(functools.partial(kernel, nd, nb), out_shape=(pltpu.VMEM((...  76.1 us

profile of v3, /device:TPU:1, one launch (start us, length us, event | category | flops | bytes accessed | tf_op | source)
XLA Modules:
  0.0 78.2 jit_solution(16361812645820357555)
XLA Ops:
  0.6 76.1 %shard_map.121 = (bf16[256,256]{1,0:T(8,128)(2,1)S(1)}, f32[8,512,128]{2,1,0:T(8,128)S(1)}, f32[32,864]{1,0:T(8,128)S(1)}) custom-call(bf16[8,512,128]{2,1,0:T(8,128)(2,1)} %bitcast.5, s32[2,16]{1,0:T(2,128)} %bitcast.8, s32[8,16,128]{2,1,0:T(8,128)} %vf_in.1, bf16[32,864]{1,0:T(8,128)(2,1)} %cw_in.1, bf16[32,256]{1,0:T(8,128)(2,1)} %emb_in.1, ...), custom_call_target="tpu_custom_call" | custom-call | tf_op jit(solution)/shard_map/pallas_call | solution.py:628
  76.8 1.4 %shard_map.122 = (bf16[256,256]{1,0:T(8,128)(2,1)}, f32[8,512,128]{2,1,0:T(8,128)}, f32[32,864]{1,0:T(8,128)}) custom-call(bf16[256,256]{1,0:T(8,128)(2,1)S(1)} %get-tuple-element.9.fo, f32[8,512,128]{2,1,0:T(8,128)S(1)} %get-tuple-element.10.gf, f32[32,864]{1,0:T(8,128)S(1)} %get-tuple-element.11.gc), custom_call_target="tpu_custom_call" | custom-call | tf_op jit(solution)/shard_map/pallas_call | solution.py:642

commit v4 on v3

--- a/solution.py
+++ b/solution.py
@@ -86,6 +86,8 @@
     wide,
     gwide,
     lohot,
+    lotall,
+    hids,
     ahot,
     ahot1,
     slopes,
@@ -226,13 +228,12 @@
     by, bz = lax.rem(b, 4), b // 4
     near = sorted(range(16), key=lambda o: min(o % 4, 4 - o % 4) + min(o // 4, 4 - o // 4))
     far = near[:0:-1]
-    owner = [4 * lax.rem(bz + 4 - o // 4, 4) + lax.rem(by + 4 - o % 4, 4) for o in near]
 
     def beam_copy(src, dst, base):
         def make(off):
             peer = 4 * lax.rem(bz + off // 4, 4) + lax.rem(by + off % 4, 4)
             return pltpu.make_async_remote_copy(
-                src_ref=src(peer),
+                src_ref=src(peer, off),
                 dst_ref=dst(off) if callable(dst) else dst,
                 send_sem=ks.at[base, off],
                 recv_sem=kr.at[base, off],
@@ -283,12 +284,20 @@
     sub_b = sub_hi.astype(F32).astype(BF16)
     one_b = jnp.ones((16, 256), BF16)
     zero_b = jnp.zeros((16, 256), BF16)
+    lane_b = lax.broadcasted_iota(jnp.int32, (256, 128), 1).astype(F32).astype(BF16)
+    one_c = jnp.ones((256, 128), BF16)
+    zero_c = jnp.zeros((256, 128), BF16)
 
     def fids(x):
         return jnp.concatenate([vf[x, 0:8, :], vf[x, 8:16, :]], axis=1)
 
+    def shift_of(x, sign):
+        hi = fids(x) >> 8
+        return ((((hi >> 2) - bz) * sign & 3) << 2) + (((hi & 3) - by) * sign & 3)
+
     def counts_of(x, total):
         ids = fids(x)
+        columns = (ids & 255).astype(F32).T
         for k in range(2):
             parts = []
             for yo in range(YB):
@@ -301,15 +310,20 @@
                     lohot[2 * x + k, j * 16 : j * 16 + 16, yo * 256 : yo * 256 + 256] = jnp.where(
                         sub_b == lo_b - BF16(16 * j), one_b, zero_b
                     )
+                col = jnp.broadcast_to(columns[:, r : r + 1], (256, 128)).astype(BF16)
+                for j in range(2):
+                    lotall[2 * x + k, yo * 256 : yo * 256 + 256, j * 128 : j * 128 + 128] = jnp.where(
+                        col == lane_b + BF16(128 * j), one_c, zero_c
+                    )
                 parts.append(jnp.where(sub_hi == hi, mrow, 0.0).astype(BF16))
-            total = total + mm(jnp.concatenate(parts, axis=1), lohot[2 * x + k], NT)
+            total = total + mm(jnp.concatenate(parts, axis=1), lotall[2 * x + k], NN)
         return total
 
     counts = lax.fori_loop(0, 8, counts_of, jnp.zeros((16, 256), F32))
     for j in range(16):
         cs[j] = jnp.broadcast_to(counts[j : j + 1, :], (8, 256))
     cr[b] = cs[b]
-    count_copies = beam_copy(lambda peer: cs.at[peer], cr.at[b], 0)
+    count_copies = beam_copy(lambda peer, off: cs.at[peer], cr.at[b], 0)
     start_all(count_copies, nb)
 
     widen(wide, cw)
@@ -325,8 +339,16 @@
 
     zero_h = jnp.zeros((C, 256), BF16)
 
+    def fill(hot, r, shifts, hid, first, last):
+        yo = r % YB
+        row = jnp.broadcast_to(shifts[r : r + 1, :], (C, 256)).astype(F32).astype(BF16)
+        for p in range(first, last):
+            hot[p * C : p * C + C, yo * 256 : yo * 256 + 256] = jnp.where(
+                row == BF16(near[p]), hid, zero_h
+            )
+
     def convolve(x, k, hot):
-        ids = fids(x)
+        shifts = shift_of(x, 1)
         start = pl.multiple_of(x * WIN, C)
         conv = mm(wide[...], cols[pl.ds(start, KC), k * 256 : k * 256 + 256], NN)
         slopes[2 * x + k] = conv
@@ -335,33 +357,46 @@
             at = pl.multiple_of((x + 1) * WIN + (yo + 1) * 96 + C, C)
             act = cols[pl.ds(at, C), k * 256 : k * 256 + 256].astype(F32)
             hid = (mrow * (act + silu[yo * C : yo * C + C, :])).astype(BF16)
-            r = k * YB + yo
-            hi = jnp.broadcast_to(ids[r : r + 1, :] >> 8, (C, 256)).astype(F32).astype(BF16)
-            for q in range(16):
-                hot[q * C : q * C + C, yo * 256 : yo * 256 + 256] = jnp.where(
-                    hi == BF16(q), hid, zero_h
-                )
-
-    def scatter(g, hot):
-        sums[...] += mm(hot[...], lohot[g], NT)
-
-    def forward(x, carry):
-        scatter(2 * x, ahot)
-        convolve(x, 1, ahot1)
-        scatter(2 * x + 1, ahot1)
-        convolve(x + 1, 0, ahot)
-        return carry
-
-    convolve(0, 0, ahot)
-    lax.fori_loop(0, 7, forward, 0)
-    scatter(14, ahot)
-    convolve(7, 1, ahot1)
-    scatter(15, ahot1)
-    for j in range(16):
-        ms[j] = sums[j * C : j * C + C, :].astype(BF16)
-    mr[b] = ms[b]
-    sum_copies = beam_copy(lambda peer: ms.at[peer], mr.at[b], 1)
-    start_all(sum_copies, nb)
+            hids[2 * x + k, yo * C : yo * C + C, :] = hid
+            fill(hot, k * YB + yo, shifts, hid, NEAR, 16)
+
+    def refill(x, k, hot):
+        shifts = shift_of(x, 1)
+        for yo in range(YB):
+            fill(hot, k * YB + yo, shifts, hids[2 * x + k, yo * C : yo * C + C, :], 0, NEAR)
+
+    def scatter_far(g, hot):
+        sums[NEAR * C : 512, :] += mm(hot[NEAR * C : 512, :], lotall[g], NN)
+
+    def scatter_near(g, hot):
+        sums[0 : NEAR * C, :] += mm(hot[0 : NEAR * C, :], lotall[g], NN)
+
+    def two_stage(make, use):
+        def step(x, carry):
+            use(2 * x, ahot)
+            make(x, 1, ahot1)
+            use(2 * x + 1, ahot1)
+            make(x + 1, 0, ahot)
+            return carry
+
+        make(0, 0, ahot)
+        lax.fori_loop(0, 7, step, 0)
+        use(14, ahot)
+        make(7, 1, ahot1)
+        use(15, ahot1)
+
+    sum_copies = beam_copy(
+        lambda peer, off: ms.at[near.index(off)], lambda off: mr.at[near.index(off)], 1
+    )
+    two_stage(convolve, scatter_far)
+    for p in range(15, NEAR - 1, -1):
+        ms[p] = sums[p * C : p * C + C, :].astype(BF16)
+        sum_copies(near[p]).start()
+    two_stage(refill, scatter_near)
+    for p in range(NEAR - 1, 0, -1):
+        ms[p] = sums[p * C : p * C + C, :].astype(BF16)
+        sum_copies(near[p]).start()
+    mr[0] = sums[0:C, :].astype(BF16)
 
     def slope_of(g, carry):
         sig = 1.0 / (1.0 + jnp.exp(-slopes[g]))
@@ -388,7 +423,7 @@
     inverse = 1.0 / jnp.maximum(number[0:1, :], 1.0)
     pooled = (total * inverse).astype(BF16)
     pa[b] = pooled
-    pool_copies = beam_copy(lambda peer: pa.at[b], pa.at[b], 2)
+    pool_copies = beam_copy(lambda peer, off: pa.at[b], pa.at[b], 2)
     start_all(pool_copies, nb)
 
     pre_own = mm(pooled, emb[...], TN)
@@ -415,7 +450,7 @@
     for j in range(16):
         ms2[j] = back_sums[j * C : j * C + C, :].astype(BF16)
     mr2[b] = ms2[b]
-    back_copies = beam_copy(lambda peer: ms2.at[peer], mr2.at[b], 3)
+    back_copies = beam_copy(lambda peer, off: ms2.at[peer], mr2.at[b], 3)
     start_all(back_copies, nb)
 
     gathered = mm(dst_hot, silu_msg.astype(BF16), NT).astype(BF16)
@@ -426,23 +461,23 @@
     for j in range(16):
         remote = remote + mr2[j].astype(F32)
     bm[0] = (remote * inverse).astype(BF16)
-    mean_copies = beam_copy(lambda peer: bm.at[0], lambda off: bm.at[near.index(off)], 4)
+    mean_copies = beam_copy(lambda peer, off: bm.at[0], lambda off: bm.at[near.index(off)], 4)
     start_all(mean_copies, nb)
     gbig[...] = jnp.zeros_like(gbig)
     for off in near[1:NEAR]:
         mean_copies(off).wait()
 
     def gather_near(x, carry):
-        ids = fids(x)
+        shifts = shift_of(x, -1)
         means = bm[0:NEAR].reshape(NEAR * C, 256)
         for k in range(2):
             for yo in range(YB):
                 r = k * YB + yo
-                hi = ids[r : r + 1, :] >> 8
+                hi = shifts[r : r + 1, :]
                 res[0 : NEAR * C, :] = mm(means, lohot[2 * x + k, :, yo * 256 : yo * 256 + 256], NN)
                 hid = res[0:C, :]
                 for q in range(1, NEAR):
-                    hid = jnp.where(hi == owner[q], res[q * C : q * C + C, :], hid)
+                    hid = jnp.where(hi == near[q], res[q * C : q * C + C, :], hid)
                 bh[2 * x + k, yo * C : yo * C + C, :] = hid.astype(BF16)
         return carry
 
@@ -454,17 +489,17 @@
         means = bm[NEAR:16].reshape((16 - NEAR) * C, 256)
         for j in range(2):
             x = 2 * i + j
-            ids = fids(x)
+            shifts = shift_of(x, -1)
             for k in range(2):
                 g = 2 * x + k
                 for yo in range(YB):
                     r = k * YB + yo
-                    hi = ids[r : r + 1, :] >> 8
+                    hi = shifts[r : r + 1, :]
                     got = mm(means, lohot[g, :, yo * 256 : yo * 256 + 256], NN)
                     hid = bh[g, yo * C : yo * C + C, :].astype(F32)
                     for q in range(NEAR, 16):
                         at = (q - NEAR) * C
-                        hid = jnp.where(hi == owner[q], got[at : at + C, :], hid)
+                        hid = jnp.where(hi == near[q], got[at : at + C, :], hid)
                     bh[g, yo * C : yo * C + C, :] = hid.astype(BF16)
                     back = hid * slopes[g, yo * C : yo * C + C, :]
                     row = j * YB * C + yo * C
@@ -534,7 +569,7 @@
     for j in range(1, 8):
         part = part + g1[j]
     g2[b] = part.astype(BF16)
-    second = beam_copy(lambda peer: g2.at[b], g2.at[b], 5)
+    second = beam_copy(lambda peer, off: g2.at[b], g2.at[b], 5)
     start_all(second, nb)
     for copy in back_halos:
         copy.wait()
@@ -590,6 +625,8 @@
         pltpu.VMEM((YB * C, KC), BF16),
         pltpu.VMEM((YB * C, KC), BF16),
         pltpu.VMEM((16, 256, 1024), BF16),
+        pltpu.VMEM((16, 1024, 256), BF16),
+        pltpu.VMEM((16, YB * C, 256), BF16),
         pltpu.VMEM((512, 1024), BF16),
         pltpu.VMEM((512, 1024), BF16),
         pltpu.VMEM((16, YB * C, 256), F32),
@@ -636,7 +673,7 @@
         out_specs=(vmem, vmem, vmem),
         scratch_shapes=scratch,
         compiler_params=pltpu.CompilerParams(
-            collective_id=0, has_side_effects=True, vmem_limit_bytes=48 << 20
+            collective_id=0, has_side_effects=True, vmem_limit_bytes=57 << 20
         ),
     )(*[pltpu.with_memory_space_constraint(one, pltpu.HBM) for one in inputs])
     fo, gf, gc = pl.pallas_call(

time: 78.3 us -> 77.3 us (0.987)
  Pallas kernels: 77.5 us -> 76.5 us
    pallas_call x1, Pallas kernels: 76.1 us -> 75.1 us  [body(): pl.pallas_call(functools.partial(kernel, nd, nb), out_shape=(pltpu.VMEM((...]
where the time goes in v4:
time: 77.3 us; the launch traced here: 77.2 us
  Pallas kernels  76.5 us (99%)
    pallas_call x1, Pallas kernels, body(): pl.pallas_call(functools.partial(kernel, nd, nb), out_shape=(pltpu.VMEM((...  75.1 us

profile of v4, /device:TPU:1, one launch (start us, length us, event | category | flops | bytes accessed | tf_op | source)
XLA Modules:
  0.0 77.2 jit_solution(17304237618039567626)
XLA Ops:
  0.6 75.1 %shard_map.121 = (bf16[256,256]{1,0:T(8,128)(2,1)S(1)}, f32[8,512,128]{2,1,0:T(8,128)S(1)}, f32[32,864]{1,0:T(8,128)S(1)}) custom-call(bf16[8,512,128]{2,1,0:T(8,128)(2,1)} %bitcast.5, s32[2,16]{1,0:T(2,128)} %bitcast.8, s32[8,16,128]{2,1,0:T(8,128)} %vf_in.1, bf16[32,864]{1,0:T(8,128)(2,1)} %cw_in.1, bf16[32,256]{1,0:T(8,128)(2,1)} %emb_in.1, ...), custom_call_target="tpu_custom_call" | custom-call | tf_op jit(solution)/shard_map/pallas_call | solution.py:665
  75.8 1.4 %shard_map.122 = (bf16[256,256]{1,0:T(8,128)(2,1)}, f32[8,512,128]{2,1,0:T(8,128)}, f32[32,864]{1,0:T(8,128)}) custom-call(bf16[256,256]{1,0:T(8,128)(2,1)S(1)} %get-tuple-element.9.fo, f32[8,512,128]{2,1,0:T(8,128)S(1)} %get-tuple-element.10.gf, f32[32,864]{1,0:T(8,128)S(1)} %get-tuple-element.11.gc), custom_call_target="tpu_custom_call" | custom-call | tf_op jit(solution)/shard_map/pallas_call | solution.py:679

commit v5 on v4

--- a/solution.py
+++ b/solution.py
@@ -15,6 +15,8 @@
 WIN = (YB + 2) * 3 * C
 KC = 3 * WIN
 NEAR = 11
+CLOSE = 5
+EC = 1
 NN = (((1,), (0,)), ((), ()))
 NT = (((1,), (1,)), ((), ()))
 TN = (((0,), (0,)), ((), ()))
@@ -94,7 +96,6 @@
     bh,
     bc,
     bc1,
-    res,
     sums,
     gbig,
     hx,
@@ -164,8 +165,8 @@
         greet(dev)
     for copy in loads:
         copy.start()
-    for copy in loads:
-        copy.wait()
+    loads[0].wait()
+    loads[1].wait()
 
     lane = lax.broadcasted_iota(jnp.int32, (C, 128), 1)
     square = (C, C)
@@ -295,37 +296,28 @@
         hi = fids(x) >> 8
         return ((((hi >> 2) - bz) * sign & 3) << 2) + (((hi & 3) - by) * sign & 3)
 
-    def counts_of(x, total):
-        ids = fids(x)
-        columns = (ids & 255).astype(F32).T
+    def one_hots(x, carry):
+        ids = fids(x) & 255
+        columns = ids.astype(F32).T
         for k in range(2):
-            parts = []
             for yo in range(YB):
                 r = k * YB + yo
-                one = ids[r : r + 1, :]
-                lo = one & 255
-                hi = one >> 8
-                lo_b = jnp.broadcast_to(lo, (16, 256)).astype(F32).astype(BF16)
-                for j in range(16):
-                    lohot[2 * x + k, j * 16 : j * 16 + 16, yo * 256 : yo * 256 + 256] = jnp.where(
-                        sub_b == lo_b - BF16(16 * j), one_b, zero_b
-                    )
                 col = jnp.broadcast_to(columns[:, r : r + 1], (256, 128)).astype(BF16)
                 for j in range(2):
                     lotall[2 * x + k, yo * 256 : yo * 256 + 256, j * 128 : j * 128 + 128] = jnp.where(
                         col == lane_b + BF16(128 * j), one_c, zero_c
                     )
-                parts.append(jnp.where(sub_hi == hi, mrow, 0.0).astype(BF16))
-            total = total + mm(jnp.concatenate(parts, axis=1), lotall[2 * x + k], NN)
-        return total
-
-    counts = lax.fori_loop(0, 8, counts_of, jnp.zeros((16, 256), F32))
-    for j in range(16):
-        cs[j] = jnp.broadcast_to(counts[j : j + 1, :], (8, 256))
-    cr[b] = cs[b]
-    count_copies = beam_copy(lambda peer, off: cs.at[peer], cr.at[b], 0)
-    start_all(count_copies, nb)
-
+                lo_b = jnp.broadcast_to(ids[r : r + 1, :], (16, 256)).astype(F32).astype(BF16)
+                for j in range(16):
+                    lohot[2 * x + k, j * 16 : j * 16 + 16, yo * 256 : yo * 256 + 256] = jnp.where(
+                        sub_b == lo_b - BF16(16 * j), one_b, zero_b
+                    )
+        return carry
+
+    loads[3].wait()
+    lax.fori_loop(0, 8, one_hots, 0)
+
+    loads[2].wait()
     widen(wide, cw)
     turned = mm(cw[...], eye, TN)
     for t in range(27):
@@ -349,6 +341,7 @@
 
     def convolve(x, k, hot):
         shifts = shift_of(x, 1)
+        owners = fids(x) >> 8
         start = pl.multiple_of(x * WIN, C)
         conv = mm(wide[...], cols[pl.ds(start, KC), k * 256 : k * 256 + 256], NN)
         slopes[2 * x + k] = conv
@@ -358,7 +351,11 @@
             act = cols[pl.ds(at, C), k * 256 : k * 256 + 256].astype(F32)
             hid = (mrow * (act + silu[yo * C : yo * C + C, :])).astype(BF16)
             hids[2 * x + k, yo * C : yo * C + C, :] = hid
-            fill(hot, k * YB + yo, shifts, hid, NEAR, 16)
+            r = k * YB + yo
+            fill(hot, r, shifts, hid, NEAR, 16)
+            hot[512:528, yo * 256 : yo * 256 + 256] = jnp.where(
+                sub_hi == owners[r : r + 1, :], mrow, 0.0
+            ).astype(BF16)
 
     def refill(x, k, hot):
         shifts = shift_of(x, 1)
@@ -366,7 +363,7 @@
             fill(hot, k * YB + yo, shifts, hids[2 * x + k, yo * C : yo * C + C, :], 0, NEAR)
 
     def scatter_far(g, hot):
-        sums[NEAR * C : 512, :] += mm(hot[NEAR * C : 512, :], lotall[g], NN)
+        sums[NEAR * C : 528, :] += mm(hot[NEAR * C : 528, :], lotall[g], NN)
 
     def scatter_near(g, hot):
         sums[0 : NEAR * C, :] += mm(hot[0 : NEAR * C, :], lotall[g], NN)
@@ -392,6 +389,11 @@
     for p in range(15, NEAR - 1, -1):
         ms[p] = sums[p * C : p * C + C, :].astype(BF16)
         sum_copies(near[p]).start()
+    for j in range(16):
+        cs[j] = jnp.broadcast_to(sums[512 + j : 513 + j, :], (8, 256))
+    cr[b] = cs[b]
+    count_copies = beam_copy(lambda peer, off: cs.at[peer], cr.at[b], 0)
+    start_all(count_copies, nb)
     two_stage(refill, scatter_near)
     for p in range(NEAR - 1, 0, -1):
         ms[p] = sums[p * C : p * C + C, :].astype(BF16)
@@ -405,6 +407,8 @@
 
     lax.fori_loop(0, 16, slope_of, 0)
 
+    for i in range(4, 10):
+        loads[i].wait()
     sub_e = lax.broadcasted_iota(jnp.int32, (256, 1024), 0)
     src = es[...]
     src_lo = (sub_e == (src & 255)).astype(F32).astype(BF16)
@@ -433,27 +437,34 @@
 
     wait_all(pool_copies, nb)
     table = pa[...].reshape(16 * C, 256)
-    picked = jnp.zeros((C, 1024), F32)
-    every = mm(table, src_lo, NN)
-    for q in range(16):
-        picked = jnp.where(src_hi == q, every[q * C : q * C + C, :], picked)
-    pre_src = mm(emb[...], picked.astype(BF16), TN)
-    silu_src, slope_src = sig_parts(pre_src)
-    pre_msg = mm(mw[...], silu_src.astype(BF16), TN)
-    silu_msg, slope_msg = sig_parts(pre_msg)
-    back_pre = (agg_edge * slope_msg).astype(BF16)
-    back_src = mm(mw[...], back_pre, NN)
-    back_edge = mm(emb[...], (back_src * slope_src).astype(BF16), NN)
-    for q in range(16):
-        ahot[q * C : q * C + C, :] = jnp.where(src_hi == q, back_edge, 0.0).astype(BF16)
-    back_sums = mm(ahot[...], src_lo, NT)
+    msgs = []
+    for e in range(EC):
+        w = 1024 // EC
+        cut = slice(e * w, e * w + w)
+        every = mm(table, src_lo[:, cut], NN)
+        picked = every[0:C, :]
+        for q in range(1, 16):
+            picked = jnp.where(src_hi[:, cut] == q, every[q * C : q * C + C, :], picked)
+        pre_src = mm(emb[...], picked.astype(BF16), TN)
+        silu_src, slope_src = sig_parts(pre_src)
+        pre_msg = mm(mw[...], silu_src.astype(BF16), TN)
+        silu_msg, slope_msg = sig_parts(pre_msg)
+        msgs.append(silu_msg.astype(BF16))
+        back_pre = (agg_edge[:, cut] * slope_msg).astype(BF16)
+        back_src = mm(mw[...], back_pre, NN)
+        back_edge = mm(emb[...], (back_src * slope_src).astype(BF16), NN)
+        for q in range(16):
+            ahot[q * C : q * C + C, cut] = jnp.where(src_hi[:, cut] == q, back_edge, 0.0).astype(
+                BF16
+            )
+    back_sums = mm(ahot[0:512, :], src_lo, NT)
     for j in range(16):
         ms2[j] = back_sums[j * C : j * C + C, :].astype(BF16)
     mr2[b] = ms2[b]
     back_copies = beam_copy(lambda peer, off: ms2.at[peer], mr2.at[b], 3)
     start_all(back_copies, nb)
 
-    gathered = mm(dst_hot, silu_msg.astype(BF16), NT).astype(BF16)
+    gathered = mm(dst_hot, jnp.concatenate(msgs, axis=1), NT).astype(BF16)
     fo[...] = (own.astype(F32) + mm(gathered, uw[...], NN)).astype(BF16)
 
     wait_all(back_copies, nb)
@@ -462,31 +473,32 @@
         remote = remote + mr2[j].astype(F32)
     bm[0] = (remote * inverse).astype(BF16)
     mean_copies = beam_copy(lambda peer, off: bm.at[0], lambda off: bm.at[near.index(off)], 4)
-    start_all(mean_copies, nb)
+    for off in near[1:]:
+        mean_copies(off).start()
     gbig[...] = jnp.zeros_like(gbig)
-    for off in near[1:NEAR]:
+    for off in near[1:CLOSE]:
         mean_copies(off).wait()
 
     def gather_near(x, carry):
         shifts = shift_of(x, -1)
-        means = bm[0:NEAR].reshape(NEAR * C, 256)
+        means = bm[0:CLOSE].reshape(CLOSE * C, 256)
         for k in range(2):
             for yo in range(YB):
                 r = k * YB + yo
                 hi = shifts[r : r + 1, :]
-                res[0 : NEAR * C, :] = mm(means, lohot[2 * x + k, :, yo * 256 : yo * 256 + 256], NN)
-                hid = res[0:C, :]
-                for q in range(1, NEAR):
-                    hid = jnp.where(hi == near[q], res[q * C : q * C + C, :], hid)
+                got = mm(means, lohot[2 * x + k, :, yo * 256 : yo * 256 + 256], NN)
+                hid = got[0:C, :]
+                for q in range(1, CLOSE):
+                    hid = jnp.where(hi == near[q], got[q * C : q * C + C, :], hid)
                 bh[2 * x + k, yo * C : yo * C + C, :] = hid.astype(BF16)
         return carry
 
     lax.fori_loop(0, 8, gather_near, 0)
-    for off in near[NEAR:]:
+    for off in near[CLOSE:]:
         mean_copies(off).wait()
 
     def gather_far(i, out):
-        means = bm[NEAR:16].reshape((16 - NEAR) * C, 256)
+        means = bm[CLOSE:16].reshape((16 - CLOSE) * C, 256)
         for j in range(2):
             x = 2 * i + j
             shifts = shift_of(x, -1)
@@ -497,8 +509,8 @@
                     hi = shifts[r : r + 1, :]
                     got = mm(means, lohot[g, :, yo * 256 : yo * 256 + 256], NN)
                     hid = bh[g, yo * C : yo * C + C, :].astype(F32)
-                    for q in range(NEAR, 16):
-                        at = (q - NEAR) * C
+                    for q in range(CLOSE, 16):
+                        at = (q - CLOSE) * C
                         hid = jnp.where(hi == near[q], got[at : at + C, :], hid)
                     bh[g, yo * C : yo * C + C, :] = hid.astype(BF16)
                     back = hid * slopes[g, yo * C : yo * C + C, :]
@@ -627,14 +639,13 @@
         pltpu.VMEM((16, 256, 1024), BF16),
         pltpu.VMEM((16, 1024, 256), BF16),
         pltpu.VMEM((16, YB * C, 256), BF16),
-        pltpu.VMEM((512, 1024), BF16),
-        pltpu.VMEM((512, 1024), BF16),
+        pltpu.VMEM((528, 1024), BF16),
+        pltpu.VMEM((528, 1024), BF16),
         pltpu.VMEM((16, YB * C, 256), F32),
         pltpu.VMEM((16, YB * C, 256), BF16),
         pltpu.VMEM((2 * YB * C, 512), BF16),
         pltpu.VMEM((2 * YB * C, 512), BF16),
-        pltpu.VMEM((512, 256), F32),
-        pltpu.VMEM((512, 256), F32),
+        pltpu.VMEM((528, 256), F32),
         pltpu.VMEM((4 * WIN, 256), F32),
         pltpu.VMEM((2, 512, 128), BF16),
         pltpu.VMEM((2, 8, C, 128), BF16),

time: 77.3 us -> 75 us (0.970)
  Pallas kernels: 76.5 us -> 74.2 us
    pallas_call x1, Pallas kernels: 75.1 us -> 72.8 us  [body(): pl.pallas_call(functools.partial(kernel, nd, nb), out_shape=(pltpu.VMEM((...]
where the time goes in v5:
time: 75 us; the launch traced here: 74.9 us
  Pallas kernels  74.2 us (99%)
    pallas_call x1, Pallas kernels, body(): pl.pallas_call(functools.partial(kernel, nd, nb), out_shape=(pltpu.VMEM((...  72.8 us

profile of v5, /device:TPU:1, one launch (start us, length us, event | category | flops | bytes accessed | tf_op | source)
XLA Modules:
  0.0 74.9 jit_solution(14905553021011085550)
XLA Ops:
  0.6 72.8 %shard_map.121 = (bf16[256,256]{1,0:T(8,128)(2,1)S(1)}, f32[8,512,128]{2,1,0:T(8,128)S(1)}, f32[32,864]{1,0:T(8,128)S(1)}) custom-call(bf16[8,512,128]{2,1,0:T(8,128)(2,1)} %bitcast.5, s32[2,16]{1,0:T(2,128)} %bitcast.8, s32[8,16,128]{2,1,0:T(8,128)} %vf_in.1, bf16[32,864]{1,0:T(8,128)(2,1)} %cw_in.1, bf16[32,256]{1,0:T(8,128)(2,1)} %emb_in.1, ...), custom_call_target="tpu_custom_call" | custom-call | tf_op jit(solution)/shard_map/pallas_call | solution.py:676
  73.5 1.4 %shard_map.122 = (bf16[256,256]{1,0:T(8,128)(2,1)}, f32[8,512,128]{2,1,0:T(8,128)}, f32[32,864]{1,0:T(8,128)}) custom-call(bf16[256,256]{1,0:T(8,128)(2,1)S(1)} %get-tuple-element.9.fo, f32[8,512,128]{2,1,0:T(8,128)S(1)} %get-tuple-element.10.gf, f32[32,864]{1,0:T(8,128)S(1)} %get-tuple-element.11.gc), custom_call_target="tpu_custom_call" | custom-call | tf_op jit(solution)/shard_map/pallas_call | solution.py:690

commit v6 on v5

--- a/solution.py
+++ b/solution.py
@@ -14,8 +14,8 @@
 YB = 4
 WIN = (YB + 2) * 3 * C
 KC = 3 * WIN
-NEAR = 11
-CLOSE = 5
+NEAR = 9
+CLOSE = 6
 EC = 1
 NN = (((1,), (0,)), ((), ()))
 NT = (((1,), (1,)), ((), ()))
@@ -27,7 +27,7 @@
 
 
 def sig_parts(value):
-    sig = 1.0 / (1.0 + jnp.exp(-value))
+    sig = 0.5 + 0.5 * jnp.tanh(0.5 * value)
     return value * sig, sig * (1.0 + value * (1.0 - sig))
 
 
@@ -345,7 +345,8 @@
         start = pl.multiple_of(x * WIN, C)
         conv = mm(wide[...], cols[pl.ds(start, KC), k * 256 : k * 256 + 256], NN)
         slopes[2 * x + k] = conv
-        silu = conv / (1.0 + jnp.exp(-conv))
+        half = 0.5 * conv
+        silu = half + half * jnp.tanh(half)
         for yo in range(YB):
             at = pl.multiple_of((x + 1) * WIN + (yo + 1) * 96 + C, C)
             act = cols[pl.ds(at, C), k * 256 : k * 256 + 256].astype(F32)
@@ -401,7 +402,7 @@
     mr[0] = sums[0:C, :].astype(BF16)
 
     def slope_of(g, carry):
-        sig = 1.0 / (1.0 + jnp.exp(-slopes[g]))
+        sig = 0.5 + 0.5 * jnp.tanh(0.5 * slopes[g])
         slopes[g] = mrow * (sig * (1.0 + slopes[g] * (1.0 - sig)))
         return carry
 
@@ -461,7 +462,7 @@
     for j in range(16):
         ms2[j] = back_sums[j * C : j * C + C, :].astype(BF16)
     mr2[b] = ms2[b]
-    back_copies = beam_copy(lambda peer, off: ms2.at[peer], mr2.at[b], 3)
+    back_copies = beam_copy(lambda peer, off: ms2.at[peer], mr2.at[b], 1)
     start_all(back_copies, nb)
 
     gathered = mm(dst_hot, jnp.concatenate(msgs, axis=1), NT).astype(BF16)
@@ -472,7 +473,7 @@
     for j in range(16):
         remote = remote + mr2[j].astype(F32)
     bm[0] = (remote * inverse).astype(BF16)
-    mean_copies = beam_copy(lambda peer, off: bm.at[0], lambda off: bm.at[near.index(off)], 4)
+    mean_copies = beam_copy(lambda peer, off: bm.at[0], lambda off: bm.at[near.index(off)], 2)
     for off in near[1:]:
         mean_copies(off).start()
     gbig[...] = jnp.zeros_like(gbig)
@@ -581,7 +582,7 @@
     for j in range(1, 8):
         part = part + g1[j]
     g2[b] = part.astype(BF16)
-    second = beam_copy(lambda peer, off: g2.at[b], g2.at[b], 5)
+    second = beam_copy(lambda peer, off: g2.at[b], g2.at[b], 1)
     start_all(second, nb)
     for copy in back_halos:
         copy.wait()
@@ -668,8 +669,8 @@
         pltpu.VMEM((nd, 16, 256), F32),
         pltpu.SemaphoreType.DMA((16,)),
         pltpu.SemaphoreType.DMA((16,)),
-        pltpu.SemaphoreType.DMA((6, nb)),
-        pltpu.SemaphoreType.DMA((6, nb)),
+        pltpu.SemaphoreType.DMA((3, nb)),
+        pltpu.SemaphoreType.DMA((3, nb)),
         pltpu.SemaphoreType.DMA((2, nd)),
         pltpu.SemaphoreType.DMA((2, nd)),
     ]

time: 75 us -> 73.8 us (0.984)
  Pallas kernels: 74.2 us -> 73 us
    pallas_call x1, Pallas kernels: 72.8 us -> 71.6 us  [body(): pl.pallas_call(functools.partial(kernel, nd, nb), out_shape=(pltpu.VMEM((...]
where the time goes in v6:
time: 73.8 us; the launch traced here: 73.6 us
  Pallas kernels  73 us (99%)
    pallas_call x1, Pallas kernels, body(): pl.pallas_call(functools.partial(kernel, nd, nb), out_shape=(pltpu.VMEM((...  71.6 us

profile of v6, /device:TPU:1, one launch (start us, length us, event | category | flops | bytes accessed | tf_op | source)
XLA Modules:
  0.0 73.6 jit_solution(10490185094304409814)
XLA Ops:
  0.6 71.6 %shard_map.121 = (bf16[256,256]{1,0:T(8,128)(2,1)S(1)}, f32[8,512,128]{2,1,0:T(8,128)S(1)}, f32[32,864]{1,0:T(8,128)S(1)}) custom-call(bf16[8,512,128]{2,1,0:T(8,128)(2,1)} %bitcast.5, s32[2,16]{1,0:T(2,128)} %bitcast.8, s32[8,16,128]{2,1,0:T(8,128)} %vf_in.1, bf16[32,864]{1,0:T(8,128)(2,1)} %cw_in.1, bf16[32,256]{1,0:T(8,128)(2,1)} %emb_in.1, ...), custom_call_target="tpu_custom_call" | custom-call | tf_op jit(solution)/shard_map/pallas_call | solution.py:677
  72.2 1.4 %shard_map.122 = (bf16[256,256]{1,0:T(8,128)(2,1)}, f32[8,512,128]{2,1,0:T(8,128)}, f32[32,864]{1,0:T(8,128)}) custom-call(bf16[256,256]{1,0:T(8,128)(2,1)S(1)} %get-tuple-element.9.fo, f32[8,512,128]{2,1,0:T(8,128)S(1)} %get-tuple-element.10.gf, f32[32,864]{1,0:T(8,128)S(1)} %get-tuple-element.11.gc), custom_call_target="tpu_custom_call" | custom-call | tf_op jit(solution)/shard_map/pallas_call | solution.py:691
